TPU v7x, 1024 devices: a whole 8x8x8 slice. The times are simulated.
1024 devices in a mesh: grid: 128 (over z, x, core), mem: 8 (over y).
Axes of the slice: x: 8, y: 8, z: 8, core: 2. Of those that a mesh axis runs over, the one named last changes fastest.
Arguments:
- perturb: float32 [64, 1, 1024, 256], P('mem', None, 'grid'), may hold values from -8 to 8
- winds: float32 [2, 1, 1024, 256], P(None, None, 'grid'), may hold values from -0.6 to 0.6
- kappa: float32 [1], replicated, may hold values from 0.05 to 0.2
- obs_col: int32 [1024, 256], P('grid'), may hold values from 0 to 255
- innov: float32 [1, 1024, 256], P(None, 'grid'), may hold values from -6 to 6
- alpha: float32 [64], replicated, may hold values from -5 to 5
- loc_mask: int32 [64, 1024, 8], P('mem', 'grid'), may hold values 0 or 1
Outputs:
- factor: float32 [64, 64], replicated
- newton: float32 [64], replicated
- sens: float32 [64, 1, 1024, 256], P('mem', None, 'grid')
All inputs are finite; a program needn't handle non-finite values. No bound on the sum of `loc_mask` on one device may be relied on, other than what follows from the above.
Results may differ from a plain program's by a relative error of at most 0.000086.
Values sent between devices are 32-bit elements; how exact they have to be, the bound alone decides.
No kernel may reach another device: no remote copies, remote signals or barrier semaphores. Data moves between devices by JAX's collectives and lax.ppermute only.
A program may use at most 32 MiB of HBM per device.

v0:
```python
import jax
import jax.numpy as jnp
from jax import lax
from jax.sharding import PartitionSpec as P

STEPS = 4


def with_halo(block, sides, width):
    for axis, dim in sides:
        count = lax.axis_size(axis)
        forward = [(i, i + 1) for i in range(count - 1)]
        backward = [(target, source) for source, target in forward]
        low = lax.ppermute(
            lax.slice_in_dim(block, block.shape[dim] - width, None, axis=dim), axis, forward
        )
        high = lax.ppermute(lax.slice_in_dim(block, 0, width, axis=dim), axis, backward)
        block = jnp.concatenate([low, block, high], axis=dim)
    return block


def tangent_update(field, uwind, vwind, diffusivity):
    centre = field[..., 1:-1, :]
    east = jnp.roll(centre, -1, axis=-1)
    west = jnp.roll(centre, 1, axis=-1)
    north = field[..., 2:, :]
    south = field[..., :-2, :]
    ucen = uwind[:, 1:-1, :]
    vcen = vwind[:, 1:-1, :]
    return (
        centre
        - 0.5 * ucen * (east - west)
        - 0.5 * vcen * (north - south)
        + diffusivity * (east + west + north + south - 4.0 * centre)
    )


def adjoint_update(field, uwind, vwind, diffusivity):
    centre = field[..., 1:-1, :]
    zonal = uwind[:, 1:-1, :] * centre
    merid = vwind * field
    east = jnp.roll(centre, -1, axis=-1)
    west = jnp.roll(centre, 1, axis=-1)
    lap = east + west + field[..., 2:, :] + field[..., :-2, :] - 4.0 * centre
    advect = 0.5 * (jnp.roll(zonal, -1, axis=-1) - jnp.roll(zonal, 1, axis=-1)) + 0.5 * (
        merid[..., 2:, :] - merid[..., :-2, :]
    )
    return centre + advect + diffusivity * lap


def per_device(perturb, winds, kappa, obs_col, innov, alpha, loc_mask):
    diffusivity = kappa[:, None, None]
    local_members = perturb.shape[0]
    levels = perturb.shape[1]
    rows = perturb.shape[2]
    columns = perturb.shape[3]
    per_row = obs_col.shape[1]
    total_rows = rows * lax.axis_size("grid")
    meridional_padded = with_halo(winds[1], (("grid", 1),), 1)
    zonal_padded = jnp.pad(winds[0], ((0, 0), (1, 1), (0, 0)))
    model_state = perturb
    for step in range(STEPS):
        halo_padded = with_halo(model_state, (("grid", 2),), 1)
        model_state = tangent_update(halo_padded, zonal_padded, meridional_padded, diffusivity)
    index = jnp.broadcast_to(obs_col[None, None], (local_members, levels, rows, per_row))
    hy = jnp.take_along_axis(model_state, index, axis=3)
    moved = lax.all_to_all(hy, "mem", split_axis=3, concat_axis=0, tiled=True)
    members = moved.shape[0]
    block = moved.shape[3]
    scale = 1.0 / members**0.5
    alpha_local = lax.dynamic_slice_in_dim(
        alpha, lax.axis_index("mem") * local_members, local_members, 0
    )
    partial_sum = (
        jnp.einsum("m,mlyk->lyk", alpha_local, hy, precision=lax.Precision.HIGHEST) * scale
    )
    resid = innov - lax.psum(partial_sum, "mem")
    resid_part = lax.dynamic_slice_in_dim(resid, lax.axis_index("mem") * block, block, 2)
    flat = moved.reshape(members, -1)
    gram = jnp.dot(flat, flat.T, precision=lax.Precision.HIGHEST)
    proj = jnp.dot(flat, resid_part.reshape(-1), precision=lax.Precision.HIGHEST)
    gram, proj = lax.psum((gram, proj), ("grid", "mem"))
    count = float(levels * total_rows * per_row)
    hess = jnp.eye(members, dtype=jnp.float32) + gram / count
    grad = alpha - members**0.5 * proj / count
    lower = jnp.linalg.cholesky(hess)
    factor = lower.T
    newton = jax.scipy.linalg.cho_solve((lower, True), grad)
    level_idx = jnp.arange(levels, dtype=jnp.int32)[:, None, None]
    row_idx = jnp.arange(rows, dtype=jnp.int32)[None, :, None]
    col_idx = obs_col[None]
    forcing = (
        jnp.zeros((levels, rows, columns), jnp.float32).at[level_idx, row_idx, col_idx].add(resid)
    )
    first_step = 0
    maskf = jnp.repeat(loc_mask.astype(jnp.float32), columns // loc_mask.shape[2], axis=2)
    adjoint_model = maskf[:, None] * forcing[None]
    for step in range(first_step, STEPS):
        halo_padded = with_halo(adjoint_model, (("grid", 2),), 1)
        adjoint_model = adjoint_update(halo_padded, zonal_padded, meridional_padded, diffusivity)
    return (factor, newton, adjoint_model)


def solution(mesh):
    in_specs = (
        P("mem", None, "grid", None),
        P(None, None, "grid", None),
        P(),
        P("grid", None),
        P(None, "grid", None),
        P(),
        P("mem", "grid", None),
    )
    out_specs = (P(), P(), P("mem", None, "grid", None))
    return jax.shard_map(
        per_device, mesh=mesh, in_specs=in_specs, out_specs=out_specs, check_vma=False
    )
```

profile of v0, /device:TPU:1, one launch (start us, length us, event | category | flops | bytes accessed | tf_op | source)
XLA Modules:
  0.0 404.1 jit_solution(16202669948158131333)
XLA Ops:
  0.7 1.0 fusion.87
  1.6 4.5 %collective-permute-start.1 = (f32[8,1,1,256]{3,2,0,1:T(1,128)S(1)}, f32[8,1,1,256]{3,2,0,1:T(1,128)S(1)}, u32[]{:S(2)}, u32[]{:S(2)}) collective-permute-start(f32[8,1,1,256]{3,2,0,1:T(1,128)S(1)} %get-tuple-element.90), channel_id=1, source_target_pairs={{0,8},{8,16},{16,24},{24,32},{32,40},{40,48},{48,56},{56,64},{64,7... | collective-permute-start | bytes 24584 | tf_op jit(solution)/shard_map/ppermute | solution.py:14
  6.1 12.8 %collective-permute-start = (f32[8,1,1,256]{3,2,0,1:T(1,128)S(1)}, f32[8,1,1,256]{3,2,0,1:T(1,128)S(1)}, u32[]{:S(2)}, u32[]{:S(2)}) collective-permute-start(f32[8,1,1,256]{3,2,0,1:T(1,128)S(1)} %get-tuple-element.91), channel_id=1, source_target_pairs={{8,0},{16,8},{24,16},{32,24},{40,32},{48,40},{56,48},{64,56},{72,6... | collective-permute-start | bytes 24584 | tf_op jit(solution)/shard_map/ppermute | solution.py:17
  19.7 1.9 collective-permute-start.8
  21.6 2.4 collective-permute-start.9
  25.4 0.8 fusion.86
  26.3 1.0 fusion.85
  31.0 3.2 collective-permute-start.3
  34.1 1.9 collective-permute-start.2
  36.1 3.0 collective-permute-done.2
  39.3 1.9 collective-permute-start.5
  41.3 2.4 collective-permute-start.4
  43.7 2.5 collective-permute-done.4
  46.4 1.9 collective-permute-start.7
  48.4 2.4 collective-permute-start.6
  50.9 2.5 collective-permute-done.6
  53.5 126.3 %gather_fusion = f32[16384]{0:T(1024)S(1)} fusion(f32[8,8,256]{2,1,0:T(8,128)S(1)} %add_bitcast_fusion, s32[16384]{0:T(1024)S(1)} %bitcast.96), kind=kCustom, calls=%fused_computation | custom fusion | bytes 327680 | tf_op jit(solution)/shard_map/jit(take_along_axis)/gather | solution.py:66
  180.2 10.9 %psum.22 = f32[1,8,256]{2,1,0:T(8,128)S(1)} all-reduce(f32[1,8,256]{2,1,0:T(8,128)S(1)} %fusion.43), channel_id=1, replica_groups=mesh['grid'=128,'mem'=8] {'mem'}, use_global_device_ids=true, to_apply=%region_3.4 | all-reduce | flops 2048 | bytes 16384 | tf_op jit(solution)/shard_map/psum | solution.py:77
  191.2 14.7 %scatter_custom_fusion = f32[2048]{0:T(1024)S(1)} fusion(s32[2048]{0:T(1024)S(1)} %bitcast.105, f32[2048]{0:T(1024)S(1)} %bitcast.106, f32[]{:T(128)} %constant.89.clone.1), kind=kCustom, calls=%fused_computation.122 | custom fusion | flops 2048 | bytes 8196
  206.1 3.9 collective-permute-start.11
  210.1 3.4 collective-permute-start.10
  214.1 1.1 reshape.1197
  215.2 3.3 all-to-all-start
  219.0 1.9 collective-permute-start.13
  220.9 3.6 collective-permute-start.12
  225.8 1.9 collective-permute-start.15
  227.7 4.2 %collective-permute-start.14 = (f32[8,1,1,256]{3,2,0,1:T(1,128)S(1)}, f32[8,1,1,256]{3,2,0,1:T(1,128)S(1)}, u32[]{:S(2)}, u32[]{:S(2)}) collective-permute-start(f32[8,1,1,256]{3,2,0,1:T(1,128)S(1)} %get-tuple-element.47), channel_id=1, source_target_pairs={{0,8},{8,16},{16,24},{24,32},{32,40},{40,48},{48,56},{56,64},{64,7... | collective-permute-start | bytes 24584 | tf_op jit(solution)/shard_map/ppermute | solution.py:14
  233.1 1.9 collective-permute-start.17
  235.1 4.2 %collective-permute-start.16 = (f32[8,1,1,256]{3,2,0,1:T(1,128)S(1)}, f32[8,1,1,256]{3,2,0,1:T(1,128)S(1)}, u32[]{:S(2)}, u32[]{:S(2)}) collective-permute-start(f32[8,1,1,256]{3,2,0,1:T(1,128)S(1)} %get-tuple-element.37), channel_id=1, source_target_pairs={{0,8},{8,16},{16,24},{24,32},{32,40},{40,48},{48,56},{56,64},{64,7... | collective-permute-start | bytes 24584 | tf_op jit(solution)/shard_map/ppermute | solution.py:14
  243.7 146.7 %all-reduce = (f32[64,64]{1,0:T(8,128)S(1)}, f32[64]{0:T(128)S(1)}) all-reduce(f32[64,64]{1,0:T(8,128)S(1)} %fusion.89, f32[64]{0:T(128)S(1)} %convolution_bitcast_fusion), channel_id=1, replica_groups=mesh['grid'=128,'mem'=8] {'grid','mem'}, use_global_device_ids=true, to_apply=%region_0.1 | all-reduce | flops 4160 | bytes 33280 | tf_op jit(solution)/shard_map/psum | solution.py:82
  390.5 5.8 %cholesky.20 = f32[64,64]{1,0:T(8,128)S(1)} custom-call(f32[64,64]{1,0:T(8,128)S(1)} %fusion.41), custom_call_target="Cholesky" | custom-call | tf_op jit(solution)/shard_map/jit(cholesky)/cholesky | solution.py:86
  397.6 4.9 %custom-call.10 = f32[1,64,64]{1,2,0:T(8,128)S(1)} custom-call(f32[1,64,64]{2,1,0:T(8,128)S(1)} %get-tuple-element.92), custom_call_target="InvertDiagBlocksLowerTriangular" | custom-call | tf_op jit(solution)/shard_map/jit(_cho_solve)/triangular_solve | solution.py:88
  (111 shorter events, 17.1 us)
Async XLA Ops:
  0.6 30.1 %copy-start = (f32[8,1,8,256]{3,2,1,0:T(8,128)S(1)}, f32[8,1,8,256]{3,2,1,0:T(8,128)}, u32[]{:S(2)}) copy-start(f32[8,1,8,256]{3,2,1,0:T(8,128)} %param.7) | copy-start | bytes 196612
  0.6 29.2 %copy-start.1 = (s32[8,256]{1,0:T(8,128)S(1)}, s32[8,256]{1,0:T(8,128)}, u32[]{:S(2)}) copy-start(s32[8,256]{1,0:T(8,128)} %param.10) | copy-start | bytes 24580
  1.6 29.1 %collective-permute-start.1 = (f32[8,1,1,256]{3,2,0,1:T(1,128)S(1)}, f32[8,1,1,256]{3,2,0,1:T(1,128)S(1)}, u32[]{:S(2)}, u32[]{:S(2)}) collective-permute-start(f32[8,1,1,256]{3,2,0,1:T(1,128)S(1)} %get-tuple-element.90), channel_id=1, source_target_pairs={{0,8},{8,16},{16,24},{24,32},{32,40},{40,48},{48,56},{56,64},{64,7... | collective-permute-start | bytes 24584 | tf_op jit(solution)/shard_map/ppermute | solution.py:14
  6.1 24.6 %collective-permute-start = (f32[8,1,1,256]{3,2,0,1:T(1,128)S(1)}, f32[8,1,1,256]{3,2,0,1:T(1,128)S(1)}, u32[]{:S(2)}, u32[]{:S(2)}) collective-permute-start(f32[8,1,1,256]{3,2,0,1:T(1,128)S(1)} %get-tuple-element.91), channel_id=1, source_target_pairs={{8,0},{16,8},{24,16},{32,24},{40,32},{48,40},{56,48},{64,56},{72,6... | collective-permute-start | bytes 24584 | tf_op jit(solution)/shard_map/ppermute | solution.py:17
  19.7 11.0 %collective-permute-start.8 = (f32[1,1,256]{2,1,0:T(1,128)S(1)}, f32[1,1,256]{2,1,0:T(1,128)S(1)}, u32[]{:S(2)}, u32[]{:S(2)}) collective-permute-start(f32[1,1,256]{2,1,0:T(1,128)S(1)} %get-tuple-element.98), channel_id=1, source_target_pairs={{0,8},{8,16},{16,24},{24,32},{32,40},{40,48},{48,56},{56,64},{64,7... | collective-permute-start | bytes 3080 | tf_op jit(solution)/shard_map/ppermute | solution.py:14
  21.6 9.1 %collective-permute-start.9 = (f32[1,1,256]{2,1,0:T(1,128)S(1)}, f32[1,1,256]{2,1,0:T(1,128)S(1)}, u32[]{:S(2)}, u32[]{:S(2)}) collective-permute-start(f32[1,1,256]{2,1,0:T(1,128)S(1)} %get-tuple-element.99), channel_id=1, source_target_pairs={{8,0},{16,8},{24,16},{32,24},{40,32},{48,40},{56,48},{64,56},{72,6... | collective-permute-start | bytes 3080 | tf_op jit(solution)/shard_map/ppermute | solution.py:17
  31.0 5.2 %collective-permute-start.3 = (f32[8,1,1,256]{3,2,0,1:T(1,128)S(1)}, f32[8,1,1,256]{3,2,0,1:T(1,128)S(1)}, u32[]{:S(2)}, u32[]{:S(2)}) collective-permute-start(f32[8,1,1,256]{3,2,0,1:T(1,128)S(1)} %get-tuple-element.84), channel_id=1, source_target_pairs={{0,8},{8,16},{16,24},{24,32},{32,40},{40,48},{48,56},{56,64},{64,7... | collective-permute-start | bytes 24584 | tf_op jit(solution)/shard_map/ppermute | solution.py:14
  34.1 5.0 %collective-permute-start.2 = (f32[8,1,1,256]{3,2,0,1:T(1,128)S(1)}, f32[8,1,1,256]{3,2,0,1:T(1,128)S(1)}, u32[]{:S(2)}, u32[]{:S(2)}) collective-permute-start(f32[8,1,1,256]{3,2,0,1:T(1,128)S(1)} %get-tuple-element.85), channel_id=1, source_target_pairs={{8,0},{16,8},{24,16},{32,24},{40,32},{48,40},{56,48},{64,56},{72,6... | collective-permute-start | bytes 24584 | tf_op jit(solution)/shard_map/ppermute | solution.py:17
  39.3 4.4 %collective-permute-start.5 = (f32[8,1,1,256]{3,2,0,1:T(1,128)S(1)}, f32[8,1,1,256]{3,2,0,1:T(1,128)S(1)}, u32[]{:S(2)}, u32[]{:S(2)}) collective-permute-start(f32[8,1,1,256]{3,2,0,1:T(1,128)S(1)} %get-tuple-element.78), channel_id=1, source_target_pairs={{0,8},{8,16},{16,24},{24,32},{32,40},{40,48},{48,56},{56,64},{64,7... | collective-permute-start | bytes 24584 | tf_op jit(solution)/shard_map/ppermute | solution.py:14
  41.3 5.0 %collective-permute-start.4 = (f32[8,1,1,256]{3,2,0,1:T(1,128)S(1)}, f32[8,1,1,256]{3,2,0,1:T(1,128)S(1)}, u32[]{:S(2)}, u32[]{:S(2)}) collective-permute-start(f32[8,1,1,256]{3,2,0,1:T(1,128)S(1)} %get-tuple-element.79), channel_id=1, source_target_pairs={{8,0},{16,8},{24,16},{32,24},{40,32},{48,40},{56,48},{64,56},{72,6... | collective-permute-start | bytes 24584 | tf_op jit(solution)/shard_map/ppermute | solution.py:17
  46.4 4.4 %collective-permute-start.7 = (f32[8,1,1,256]{3,2,0,1:T(1,128)S(1)}, f32[8,1,1,256]{3,2,0,1:T(1,128)S(1)}, u32[]{:S(2)}, u32[]{:S(2)}) collective-permute-start(f32[8,1,1,256]{3,2,0,1:T(1,128)S(1)} %get-tuple-element.72), channel_id=1, source_target_pairs={{0,8},{8,16},{16,24},{24,32},{32,40},{40,48},{48,56},{56,64},{64,7... | collective-permute-start | bytes 24584 | tf_op jit(solution)/shard_map/ppermute | solution.py:14
  48.4 5.0 %collective-permute-start.6 = (f32[8,1,1,256]{3,2,0,1:T(1,128)S(1)}, f32[8,1,1,256]{3,2,0,1:T(1,128)S(1)}, u32[]{:S(2)}, u32[]{:S(2)}) collective-permute-start(f32[8,1,1,256]{3,2,0,1:T(1,128)S(1)} %get-tuple-element.73), channel_id=1, source_target_pairs={{8,0},{16,8},{24,16},{32,24},{40,32},{48,40},{56,48},{64,56},{72,6... | collective-permute-start | bytes 24584 | tf_op jit(solution)/shard_map/ppermute | solution.py:17
  53.5 126.4 %copy-start.3 = (f32[64]{0:T(128)S(1)}, f32[64]{0:T(128)}, u32[]{:S(2)}) copy-start(f32[64]{0:T(128)} %param.12) | copy-start | bytes 772
  53.5 137.6 %copy-start.2 = (f32[1,8,256]{2,1,0:T(8,128)S(1)}, f32[1,8,256]{2,1,0:T(8,128)}, u32[]{:S(2)}) copy-start(f32[1,8,256]{2,1,0:T(8,128)} %param.11) | copy-start | bytes 24580
  206.1 12.4 %collective-permute-start.11 = (f32[8,1,1,256]{3,2,0,1:T(1,128)S(1)}, f32[8,1,1,256]{3,2,0,1:T(1,128)S(1)}, u32[]{:S(2)}, u32[]{:S(2)}) collective-permute-start(f32[8,1,1,256]{3,2,0,1:T(1,128)S(1)} %get-tuple-element.66), channel_id=1, source_target_pairs={{8,0},{16,8},{24,16},{32,24},{40,32},{48,40},{56,48},{64,56},{72,6... | collective-permute-start | bytes 24584 | tf_op jit(solution)/shard_map/ppermute | solution.py:17
  210.1 8.5 %collective-permute-start.10 = (f32[8,1,1,256]{3,2,0,1:T(1,128)S(1)}, f32[8,1,1,256]{3,2,0,1:T(1,128)S(1)}, u32[]{:S(2)}, u32[]{:S(2)}) collective-permute-start(f32[8,1,1,256]{3,2,0,1:T(1,128)S(1)} %get-tuple-element.67), channel_id=1, source_target_pairs={{0,8},{8,16},{16,24},{24,32},{32,40},{40,48},{48,56},{56,64},{64,7... | collective-permute-start | bytes 24584 | tf_op jit(solution)/shard_map/ppermute | solution.py:14
  215.2 25.6 %all-to-all-start = ((f32[8,1,2048]{2,1,0:T(1,128)}), f32[8,1,2048]{2,1,0:T(1,128)S(1)}, u32[]{:S(2)}, u32[]{:S(2)}) async-start(f32[8,1,2048]{2,1,0:T(1,128)} %reshape.1197), calls=%async_computation | async-start | bytes 131072 | tf_op jit(solution)/shard_map/all_to_all | solution.py:67
  219.0 5.7 %collective-permute-start.13 = (f32[8,1,1,256]{3,2,0,1:T(1,128)S(1)}, f32[8,1,1,256]{3,2,0,1:T(1,128)S(1)}, u32[]{:S(2)}, u32[]{:S(2)}) collective-permute-start(f32[8,1,1,256]{3,2,0,1:T(1,128)S(1)} %get-tuple-element.56), channel_id=1, source_target_pairs={{8,0},{16,8},{24,16},{32,24},{40,32},{48,40},{56,48},{64,56},{72,6... | collective-permute-start | bytes 24584 | tf_op jit(solution)/shard_map/ppermute | solution.py:17
  220.9 4.4 %collective-permute-start.12 = (f32[8,1,1,256]{3,2,0,1:T(1,128)S(1)}, f32[8,1,1,256]{3,2,0,1:T(1,128)S(1)}, u32[]{:S(2)}, u32[]{:S(2)}) collective-permute-start(f32[8,1,1,256]{3,2,0,1:T(1,128)S(1)} %get-tuple-element.57), channel_id=1, source_target_pairs={{0,8},{8,16},{16,24},{24,32},{32,40},{40,48},{48,56},{56,64},{64,7... | collective-permute-start | bytes 24584 | tf_op jit(solution)/shard_map/ppermute | solution.py:14
  225.8 6.2 %collective-permute-start.15 = (f32[8,1,1,256]{3,2,0,1:T(1,128)S(1)}, f32[8,1,1,256]{3,2,0,1:T(1,128)S(1)}, u32[]{:S(2)}, u32[]{:S(2)}) collective-permute-start(f32[8,1,1,256]{3,2,0,1:T(1,128)S(1)} %get-tuple-element.46), channel_id=1, source_target_pairs={{8,0},{16,8},{24,16},{32,24},{40,32},{48,40},{56,48},{64,56},{72,6... | collective-permute-start | bytes 24584 | tf_op jit(solution)/shard_map/ppermute | solution.py:17
  227.7 5.0 %collective-permute-start.14 = (f32[8,1,1,256]{3,2,0,1:T(1,128)S(1)}, f32[8,1,1,256]{3,2,0,1:T(1,128)S(1)}, u32[]{:S(2)}, u32[]{:S(2)}) collective-permute-start(f32[8,1,1,256]{3,2,0,1:T(1,128)S(1)} %get-tuple-element.47), channel_id=1, source_target_pairs={{0,8},{8,16},{16,24},{24,32},{32,40},{40,48},{48,56},{56,64},{64,7... | collective-permute-start | bytes 24584 | tf_op jit(solution)/shard_map/ppermute | solution.py:14
  233.1 6.2 %collective-permute-start.17 = (f32[8,1,1,256]{3,2,0,1:T(1,128)S(1)}, f32[8,1,1,256]{3,2,0,1:T(1,128)S(1)}, u32[]{:S(2)}, u32[]{:S(2)}) collective-permute-start(f32[8,1,1,256]{3,2,0,1:T(1,128)S(1)} %get-tuple-element.36), channel_id=1, source_target_pairs={{8,0},{16,8},{24,16},{32,24},{40,32},{48,40},{56,48},{64,56},{72,6... | collective-permute-start | bytes 24584 | tf_op jit(solution)/shard_map/ppermute | solution.py:17
  235.1 5.0 %collective-permute-start.16 = (f32[8,1,1,256]{3,2,0,1:T(1,128)S(1)}, f32[8,1,1,256]{3,2,0,1:T(1,128)S(1)}, u32[]{:S(2)}, u32[]{:S(2)}) collective-permute-start(f32[8,1,1,256]{3,2,0,1:T(1,128)S(1)} %get-tuple-element.37), channel_id=1, source_target_pairs={{0,8},{8,16},{16,24},{24,32},{32,40},{40,48},{48,56},{56,64},{64,7... | collective-permute-start | bytes 24584 | tf_op jit(solution)/shard_map/ppermute | solution.py:14
where the time goes:
time: 405 us; the launch traced here: 404 us
  blocking collectives  158 us (39%)
  local copies, waits for them, and re-layouts  135 us (33%)
  starting transfers between devices  63.8 us (16%)
  other arithmetic  33.7 us (8%)
  waiting for transfers between devices  10.1 us (2%)
    psum x1, blocking collectives, per_device(): gram, proj = lax.psum((gram, proj), ('grid', 'mem'))  147 us
    gather x3, local copies, waits for them, and re-layouts, per_device(): hy = jnp.take_along_axis(model_state, index, axis=3)  126 us
    ppermute x9, starting transfers between devices, with_halo(): lax.ppermute(lax.slice_in_dim(block, 0, width, axis=dim), axis, backward)  31.6 us
    ppermute x9, starting transfers between devices, with_halo(): lax.ppermute(lax.slice_in_dim(block, block.shape[dim] - width, None, axis...  28.9 us
    unnamed x6, other arithmetic  16.9 us
    psum x1, blocking collectives, per_device(): resid = innov - lax.psum(partial_sum, 'mem')  10.9 us
  transfers between devices with their start and end apart: 19, of which 6 were waited for; matrix products, arithmetic and copies ran while one was open for 3% of the time, Pallas kernels for 0%

commit v1 on v0

v1 whole, which is shorter than its diff:
```python
import functools

import jax
import jax.numpy as jnp
from jax import lax
from jax.experimental import pallas as pl
from jax.experimental.pallas import tpu as pltpu
from jax.sharding import Mesh
from jax.sharding import PartitionSpec as P

STEPS = 4
F32 = jnp.float32
HI = lax.Precision.HIGHEST
GRID = ("z", "x", "core")
PACK = 24


def vmem():
    return pl.BlockSpec(memory_space=pltpu.VMEM)


def call(body, outs, *args, flops=1_000_000):
    moved = sum(a.size * 4 for a in args) + sum(o.size * 4 for o in outs)
    return pl.pallas_call(
        body,
        out_shape=outs,
        in_specs=[vmem() for _ in args],
        out_specs=[vmem() for _ in outs],
        cost_estimate=pl.CostEstimate(flops=flops, bytes_accessed=moved, transcendentals=0),
        compiler_params=pltpu.CompilerParams(vmem_limit_bytes=8 * 2**20),
        name=body.__name__,
    )(*args)


def shape(*dims):
    return jax.ShapeDtypeStruct(dims, F32)


def pack_halo(field, winds, up, down):
    rows = jnp.swapaxes(field[...], 0, 1)
    down[0:4] = rows[0:4]
    up[0:4] = rows[4:8]
    down[4, 0:4, :] = winds[0:4, :]
    down[4, 4:8, :] = winds[8:12, :]
    up[4, 0:4, :] = winds[4:8, :]
    up[4, 4:8, :] = winds[12:16, :]
    down[5] = jnp.ones((8, 256), F32)
    up[5] = jnp.ones((8, 256), F32)


def bin_observations(col, innov, mask, binned, spread):
    slots = lax.broadcasted_iota(jnp.int32, (256, 256), 0)
    hit = (slots == col[...]).astype(F32)
    row = lax.broadcasted_iota(jnp.int32, (8, 256), 0)
    values = jnp.where(row == 0, 1.0, jnp.broadcast_to(innov[...], (8, 256)))
    binned[...] = lax.dot_general(
        values, hit, (((1,), (1,)), ((), ())), precision=HI, preferred_element_type=F32
    )
    block = lax.broadcasted_iota(jnp.int32, (8, 256), 1) // 32
    expand = (block == lax.broadcasted_iota(jnp.int32, (8, 256), 0)).astype(F32)
    wide = jnp.dot(mask[...].astype(F32), expand, preferred_element_type=F32)
    spread[...] = jnp.swapaxes(wide.reshape(8, 8, 256), 0, 1)


def east(x):
    return pltpu.roll(x, 255, 1)


def west(x):
    return pltpu.roll(x, 1, 1)


def wind_rows(blocks, r):
    tile = blocks[r // 4]
    u = jnp.broadcast_to(tile[4, r % 4 : r % 4 + 1, :], (8, 256))
    v = jnp.broadcast_to(tile[4, 4 + r % 4 : 5 + r % 4, :], (8, 256))
    return 0.5 * u, 0.5 * v


def tangent(low, down, up, high, kappa, out):
    blocks = (low, down, up, high)
    k = jnp.broadcast_to(kappa[...], (8, 256))
    winds = [wind_rows(blocks, r) for r in range(16)]
    rows = [blocks[r // 4][r % 4] for r in range(16)]
    for step in range(1, STEPS + 1):
        new = list(rows)
        for r in range(step, 16 - step):
            hu, hv = winds[r]
            c = rows[r]
            value = (
                (1.0 - 4.0 * k) * c
                + (k - hu) * east(c)
                + (k + hu) * west(c)
                + (k - hv) * rows[r + 1]
                + (k + hv) * rows[r - 1]
            )
            if r < 4:
                value = value * low[5]
            if r > 11:
                value = value * high[5]
            new[r] = value
        rows = new
    for y in range(8):
        out[y] = rows[4 + y]


def adjoint(low, down, up, high, plow, pdown, pup, phigh, kappa, out):
    blocks = (low, down, up, high)
    states = (plow, pdown, pup, phigh)
    k = jnp.broadcast_to(kappa[...], (8, 256))
    winds = [wind_rows(blocks, r) for r in range(16)]
    rows = [states[r // 4][r % 4] for r in range(16)]
    for step in range(1, STEPS + 1):
        new = list(rows)
        for r in range(step, 16 - step):
            hu, _ = winds[r]
            c = rows[r]
            value = (
                (1.0 - 4.0 * k) * c
                + east((k + hu) * c)
                + west((k - hu) * c)
                + (k + winds[r + 1][1]) * rows[r + 1]
                + (k - winds[r - 1][1]) * rows[r - 1]
            )
            if r < 4:
                value = value * low[5]
            if r > 11:
                value = value * high[5]
            new[r] = value
        rows = new
    out[...] = jnp.swapaxes(jnp.stack(rows[4:12], axis=0), 0, 1)


def iota2(dims, axis):
    return lax.broadcasted_iota(jnp.int32, dims, axis)


def gram_block(field, binned, alpha, out):
    copies = out.shape[0]
    x = field[...]
    count = binned[0:1, :]
    weighted = jnp.sum(alpha[...] * x, axis=0, keepdims=True) * 0.125
    forcing = binned[1:2, :] - count * weighted
    left = jnp.concatenate([x * count, jnp.broadcast_to(forcing, (8, 256))], axis=0)
    right = jnp.concatenate([x, x], axis=0)
    g = lax.dot_general(
        left, right, (((1,), (1,)), ((), ())), precision=HI, preferred_element_type=F32
    )
    lane = iota2((16, 128), 1)
    first = lane < 64
    i = iota2((16, 128), 0) + jnp.where(first, 0, 16)
    j = lane % 64
    shifted = pltpu.roll(g[32:64], 96, 1)
    top = jnp.where(first, g[0:16], g[16:32])
    low = jnp.where(first, shifted[0:16], shifted[16:32])
    packed = jnp.where((j < 32) & (i > j), low, top)
    on_diagonal = iota2((32, 128), 1) == iota2((32, 128), 0) + 96
    diagonal = jnp.sum(jnp.where(on_diagonal, g[32:64], 0.0), axis=0, keepdims=True)
    sub = iota2((8, 128), 0)
    extra = jnp.where(iota2((8, 128), 1) < 64, g[64:72], diagonal)
    tail = jnp.where(
        sub == 0,
        extra,
        jnp.where(sub == 1, forcing[:, :128], jnp.where(sub == 2, forcing[:, 128:], 0.0)),
    )
    for c in range(copies):
        out[c, 0:16, :] = packed
        out[c, 16:24, :] = tail


def sum_blocks(parts):
    total = parts[0]
    for c in range(1, parts.shape[0]):
        total = total + parts[c]
    return total


def first_sum(parts, spread, core, out, pdown, pup):
    rows = parts.shape[0] // 2
    total = parts[0:PACK, :]
    for c in range(1, parts.shape[0] // PACK):
        total = total + parts[PACK * c : PACK * c + PACK, :]
    for c in range(out.shape[0]):
        out[c] = total
    odd = core[...] > 0.5
    halves = []
    for h in range(2):
        a = parts[pl.ds(17 + h, 8, stride=PACK), :]
        b = parts[pl.ds(17 + h + rows, 8, stride=PACK), :]
        halves.append(jnp.where(odd, b, a))
    forcing = jnp.concatenate(halves, axis=1)
    for y in range(8):
        value = spread[y] * forcing[y : y + 1, :]
        if y < 4:
            pdown[y] = value
        else:
            pup[y - 4] = value


def next_sum(parts, out):
    total = sum_blocks(parts)
    for c in range(out.shape[0]):
        out[c] = total


def newton_step(count, parts, alpha, factor, newton):
    total = sum_blocks(parts)
    packed, extra = total[0:16], total[16:17]
    lane, sub = iota2((32, 128), 1), iota2((32, 128), 0)
    s = jnp.concatenate([packed, pltpu.roll(packed, 64, 1)], axis=0)
    top = jnp.where((lane >= sub) & (lane < 64), s, 0.0)
    diagonal = pltpu.roll(jnp.broadcast_to(extra, (32, 128)), 64, 1)
    bottom = jnp.where(
        lane == sub + 32,
        diagonal,
        jnp.where((lane >= 32) & (lane < sub + 32), pltpu.roll(s, 32, 1), 0.0),
    )
    z = jnp.concatenate([top, bottom, jnp.zeros((64, 128), F32)], axis=0)
    lanes, subs = iota2((64, 128), 1), iota2((64, 128), 0)
    both = z[0:64] + jnp.where(lanes == subs, 0.0, jnp.transpose(z)[0:64])
    scale = 1.0 / count
    a = jnp.where(lanes == subs, 1.0, 0.0) + both * scale
    a = jnp.where(lanes == subs + 64, 1.0, a)
    tiles = [a[8 * t : 8 * t + 8] for t in range(8)]
    sub8 = iota2((8, 128), 0)
    for k in range(64):
        t, q = divmod(k, 8)
        row = jnp.broadcast_to(tiles[t][q : q + 1, :], (8, 128))
        pivot = jnp.broadcast_to(row[:, k : k + 1], (8, 128))
        scaled = row / pivot
        for i in range(t, 8):
            mult = jnp.broadcast_to(tiles[i][:, k : k + 1], (8, 128))
            if i == t:
                mult = jnp.where(sub8 > q, mult, 0.0)
            tiles[i] = tiles[i] - mult * scaled
    u = jnp.concatenate(tiles, axis=0)
    d = jnp.sum(jnp.where(lanes == subs, u, 0.0), axis=1, keepdims=True)
    upper = jnp.where((lanes >= subs) & (lanes < 64), u, 0.0) / jnp.sqrt(d)
    factor[...] = upper[:, 0:64]
    rhs = alpha[...] - 8.0 * extra * scale
    rhs = jnp.where(iota2((1, 128), 1) < 64, rhs, 0.0)
    inverse = jnp.where(lanes >= 64, u, 0.0)
    y = jnp.sum(inverse * pltpu.roll(rhs, 64, 1), axis=1, keepdims=True) / d
    x = jnp.sum(inverse * y, axis=0, keepdims=True)
    newton[...] = pltpu.roll(x, 64, 1)[:, 0:64]


def per_device(perturb, winds, kappa, obs_col, innov, alpha, loc_mask):
    ny = lax.axis_size("y")
    blocks = lax.axis_size(GRID)
    count = float(blocks * 8 * 256)
    up, down = call(
        pack_halo,
        [shape(6, 8, 256)] * 2,
        perturb.reshape(8, 8, 256),
        winds.reshape(16, 256),
    )
    forward = [(i, i + 1) for i in range(blocks - 1)]
    backward = [(i + 1, i) for i in range(blocks - 1)]
    low = lax.ppermute(up, GRID, forward)
    high = lax.ppermute(down, GRID, backward)
    mine = lax.axis_index("y")
    core = lax.axis_index("core").astype(F32).reshape(1, 1)
    k = kappa.reshape(1, 1)
    binned, spread = call(
        bin_observations,
        [shape(8, 256), shape(8, 8, 256)],
        lax.dynamic_slice_in_dim(obs_col, mine, 1, 0),
        lax.dynamic_slice_in_dim(innov[0], mine, 1, 0),
        loc_mask.reshape(64, 8),
    )
    (evolved,) = call(tangent, [shape(8, 8, 256)], low, down, up, high, k)
    field = lax.all_to_all(evolved, "y", 0, 0, tiled=True).reshape(64, 256)
    (part,) = call(
        gram_block, [shape(2 * ny, PACK, 128)], field, binned, alpha.reshape(64, 1)
    )
    parts = lax.all_to_all(part, ("core", "y"), 0, 0, tiled=True)
    part, pdown, pup = call(
        first_sum,
        [shape(lax.axis_size("x"), PACK, 128), shape(4, 8, 256), shape(4, 8, 256)],
        parts.reshape(-1, 128),
        spread,
        core,
    )
    parts = lax.all_to_all(part, "x", 0, 0, tiled=True)
    plow = lax.ppermute(pup, GRID, forward)
    phigh = lax.ppermute(pdown, GRID, backward)
    (part,) = call(next_sum, [shape(lax.axis_size("z"), PACK, 128)], parts)
    parts = lax.all_to_all(part, "z", 0, 0, tiled=True)
    (sens,) = call(
        adjoint, [shape(8, 8, 256)], low, down, up, high, plow, pdown, pup, phigh, k
    )
    wide = jnp.concatenate([alpha, jnp.zeros((64,), F32)]).reshape(1, 128)
    final = functools.partial(newton_step, count)
    final.__name__ = "newton_step"
    factor, newton = call(final, [shape(64, 64), shape(1, 64)], parts, wide)
    return factor, newton.reshape(64), sens.reshape(8, 1, 8, 256)


def solution(mesh):
    grid, mem = mesh.devices.shape
    side = int((grid // 2) ** 0.5)
    fine = Mesh(mesh.devices.reshape(side, grid // 2 // side, 2, mem), GRID + ("y",))
    in_specs = (
        P("y", None, GRID, None),
        P(None, None, GRID, None),
        P(),
        P(GRID, None),
        P(None, GRID, None),
        P(),
        P("y", GRID, None),
    )
    out_specs = (P(), P(), P("y", None, GRID, None))
    return jax.shard_map(
        per_device, mesh=fine, in_specs=in_specs, out_specs=out_specs, check_vma=False
    )
```

time: 405 us -> 97.3 us (0.24)
  the two profiles are of different devices: /device:TPU:1 before, /device:TPU:31 now
where the time goes in v1:
time: 97.3 us; the launch traced here: 96.6 us
  starting transfers between devices  45.3 us (47%)
  waiting for transfers between devices  23.3 us (24%)
  Pallas kernels  13.5 us (14%)
  blocking collectives  10.7 us (11%)
  local copies, waits for them, and re-layouts  2.38 us (2%)
  between operations  1.4 us (1%)
    all_to_all x1, starting transfers between devices, per_device(): parts = lax.all_to_all(part, 'z', 0, 0, tiled=True)  16 us
    pallas_call x8, Pallas kernels, call(): pl.pallas_call(body, out_shape=outs, in_specs=[vmem() for _ in args], out...  13.5 us
    all_to_all x1, blocking collectives, per_device(): parts = lax.all_to_all(part, 'x', 0, 0, tiled=True)  10.7 us
    ppermute x1, starting transfers between devices, per_device(): plow = lax.ppermute(pup, GRID, forward)  9.31 us
    all_to_all x1, waiting for transfers between devices, per_device(): parts = lax.all_to_all(part, ('core', 'y'), 0, 0, tiled=True)  8.13 us
    all_to_all x1, starting transfers between devices, per_device(): field = lax.all_to_all(evolved, 'y', 0, 0, tiled=True).reshape(64, 256)  7.46 us
    ppermute x1, waiting for transfers between devices, per_device(): phigh = lax.ppermute(pdown, GRID, backward)  5.39 us
    ppermute x1, starting transfers between devices, per_device(): low = lax.ppermute(up, GRID, forward)  5.27 us
  transfers between devices with their start and end apart: 7, of which 4 were waited for; matrix products, arithmetic and copies ran while one was open for 1% of the time, Pallas kernels for 1%

profile of v1, /device:TPU:31, one launch (start us, length us, event | category | flops | bytes accessed | tf_op | source)
XLA Modules:
  0.0 96.6 jit_solution(13192402927222480801)
XLA Ops:
  0.6 0.0 copy-start
  0.6 0.0 copy-start.1
  0.7 0.8 copy-done.1
  1.5 0.0 copy-start.3
  1.5 0.7 copy-done.3
  2.2 5.3 %collective-permute-start = (f32[6,8,256]{2,1,0:T(8,128)S(1)}, f32[6,8,256]{2,1,0:T(8,128)S(1)}, u32[]{:S(2)}, u32[]{:S(2)}) collective-permute-start(f32[6,8,256]{2,1,0:T(8,128)S(1)} %get-tuple-element.12.up), channel_id=1, source_target_pairs={{0,8},{8,16},{16,24},{24,32},{32,40},{40,48},{48,56},{56,64},{64,7... | collective-permute-start | bytes 147464 | tf_op jit(solution)/shard_map/ppermute | solution.py:260
  7.5 1.9 %collective-permute-start.1 = (f32[6,8,256]{2,1,0:T(8,128)S(1)}, f32[6,8,256]{2,1,0:T(8,128)S(1)}, u32[]{:S(2)}, u32[]{:S(2)}) collective-permute-start(f32[6,8,256]{2,1,0:T(8,128)S(1)} %get-tuple-element.13.down), channel_id=1, source_target_pairs={{8,0},{16,8},{24,16},{32,24},{40,32},{48,40},{56,48},{64,56},{72,6... | collective-permute-start | bytes 147464 | tf_op jit(solution)/shard_map/ppermute | solution.py:261
  10.1 0.0 collective-permute-done.low
  10.1 4.9 %collective-permute-done.1.high = f32[6,8,256]{2,1,0:T(8,128)S(1)} collective-permute-done((f32[6,8,256]{2,1,0:T(8,128)S(1)}, f32[6,8,256]{2,1,0:T(8,128)S(1)}, u32[]{:S(2)}, u32[]{:S(2)}) %collective-permute-start.1) | collective-permute-done | bytes 49184 | tf_op jit(solution)/shard_map/ppermute | solution.py:261
  15.0 1.0 %tangent.1 = f32[8,8,256]{2,1,0:T(8,128)} custom-call(f32[6,8,256]{2,1,0:T(8,128)S(1)} %collective-permute-done.low, f32[6,8,256]{2,1,0:T(8,128)S(1)} %get-tuple-element.13.down, f32[6,8,256]{2,1,0:T(8,128)S(1)} %get-tuple-element.12.up, f32[6,8,256]{2,1,0:T(8,128)S(1)} %collective-permute-done.1.high, f32[1,1]{1,0:T(1,128)} %bitcast.16.kappa), custom_call_target="tpu_custom_call" | custom-call | flops 1000000 | bytes 262148 | tf_op jit(solution)/shard_map/tangent/pallas_call | solution.py:24
  16.1 7.5 %all-to-all-start = ((f32[8,8,256]{2,1,0:T(8,128)}), f32[8,8,256]{2,1,0:T(8,128)S(1)}, u32[]{:S(2)}, u32[]{:S(2)}) async-start(f32[8,8,256]{2,1,0:T(8,128)} %tangent.1), calls=%async_computation | async-start | bytes 131072 | tf_op jit(solution)/shard_map/all_to_all | solution.py:273
  23.5 0.0 copy-done
  23.5 0.0 copy-done.4
  23.6 0.1 copy.10.alpha
  23.7 0.7 dynamic-slice_bitcast_fusion.innov
  24.4 0.0 copy-done.2
  24.4 0.3 bin_observations.1
  24.7 4.9 %all-to-all-done = f32[8,8,256]{2,1,0:T(8,128)S(1)} async-done(((f32[8,8,256]{2,1,0:T(8,128)}), f32[8,8,256]{2,1,0:T(8,128)S(1)}, u32[]{:S(2)}, u32[]{:S(2)}) %all-to-all-start) | async-done | bytes 65568 | tf_op jit(solution)/shard_map/all_to_all | solution.py:273
  29.6 1.0 %gram_block.1 = f32[16,24,128]{2,1,0:T(8,128)} custom-call(f32[64,256]{1,0:T(8,128)S(1)} %bitcast.19, f32[8,256]{1,0:T(8,128)S(1)} %get-tuple-element.14.binned, f32[64,1]{1,0:T(8,128)S(1)} %copy.10.alpha), custom_call_target="tpu_custom_call" | custom-call | flops 1000000 | bytes 270592 | tf_op jit(solution)/shard_map/gram_block/pallas_call | solution.py:24
  30.6 3.4 %all-to-all-start.1 = ((f32[16,24,128]{2,1,0:T(8,128)}), f32[16,24,128]{2,1,0:T(8,128)S(1)}, u32[]{:S(2)}, u32[]{:S(2)}) async-start(f32[16,24,128]{2,1,0:T(8,128)} %gram_block.1), calls=%async_computation.1 | async-start | bytes 393216 | tf_op jit(solution)/shard_map/all_to_all | solution.py:277
  34.1 8.1 %all-to-all-done.1 = f32[16,24,128]{2,1,0:T(8,128)S(1)} async-done(((f32[16,24,128]{2,1,0:T(8,128)}), f32[16,24,128]{2,1,0:T(8,128)S(1)}, u32[]{:S(2)}, u32[]{:S(2)}) %all-to-all-start.1) | async-done | bytes 196640 | tf_op jit(solution)/shard_map/all_to_all | solution.py:277
  42.2 0.1 first_sum.1
  42.3 10.7 %all_to_all.20.parts = f32[8,24,128]{2,1,0:T(8,128)S(1)} all-to-all(f32[8,24,128]{2,1,0:T(8,128)S(1)} %get-tuple-element.16), channel_id=1, replica_groups=mesh['z'=8,'x'=8,'core'=2,'y'=8] {'x'}, dimensions={0} | all-to-all | bytes 196608 | tf_op jit(solution)/shard_map/all_to_all | solution.py:285
  53.0 0.7 next_sum.1
  53.6 16.0 %all-to-all-start.3 = ((f32[8,24,128]{2,1,0:T(8,128)}), f32[8,24,128]{2,1,0:T(8,128)S(1)}, u32[]{:S(2)}, u32[]{:S(2)}) async-start(f32[8,24,128]{2,1,0:T(8,128)} %next_sum.1), calls=%async_computation.3 | async-start | bytes 196608 | tf_op jit(solution)/shard_map/all_to_all | solution.py:289
  69.6 9.3 %collective-permute-start.2 = (f32[4,8,256]{2,1,0:T(8,128)S(1)}, f32[4,8,256]{2,1,0:T(8,128)S(1)}, u32[]{:S(2)}, u32[]{:S(2)}) collective-permute-start(f32[4,8,256]{2,1,0:T(8,128)S(1)} %get-tuple-element.19.pup), channel_id=1, source_target_pairs={{0,8},{8,16},{16,24},{24,32},{32,40},{40,48},{48,56},{56,64},{64,7... | collective-permute-start | bytes 98312 | tf_op jit(solution)/shard_map/ppermute | solution.py:286
  78.9 1.9 %collective-permute-start.3 = (f32[4,8,256]{2,1,0:T(8,128)S(1)}, f32[4,8,256]{2,1,0:T(8,128)S(1)}, u32[]{:S(2)}, u32[]{:S(2)}) collective-permute-start(f32[4,8,256]{2,1,0:T(8,128)S(1)} %get-tuple-element.20.pdown), channel_id=1, source_target_pairs={{8,0},{16,8},{24,16},{32,24},{40,32},{48,40},{56,48},{64,56},{72,6... | collective-permute-start | bytes 98312 | tf_op jit(solution)/shard_map/ppermute | solution.py:287
  80.8 0.0 collective-permute-done.2.plow
  80.8 5.4 %collective-permute-done.3.phigh = f32[4,8,256]{2,1,0:T(8,128)S(1)} collective-permute-done((f32[4,8,256]{2,1,0:T(8,128)S(1)}, f32[4,8,256]{2,1,0:T(8,128)S(1)}, u32[]{:S(2)}, u32[]{:S(2)}) %collective-permute-start.3) | collective-permute-done | bytes 32800 | tf_op jit(solution)/shard_map/ppermute | solution.py:287
  86.2 1.1 %adjoint.1 = f32[8,8,256]{2,1,0:T(8,128)} custom-call(f32[6,8,256]{2,1,0:T(8,128)S(1)} %collective-permute-done.low, f32[6,8,256]{2,1,0:T(8,128)S(1)} %get-tuple-element.13.down, f32[6,8,256]{2,1,0:T(8,128)S(1)} %get-tuple-element.12.up, f32[6,8,256]{2,1,0:T(8,128)S(1)} %collective-permute-done.1.high, f32[4,8,256]{2,1,0:T(8,128)S(1)} %collective-permute-done.2.plow, ...), custom_call_target="tpu_custom_call" | custom-call | flops 1000000 | bytes 393220 | tf_op jit(solution)/shard_map/adjoint/pallas_call | solution.py:24
  87.3 0.0 all-to-all-done.3.parts
  87.3 9.2 %newton_step.1 = (f32[64,64]{1,0:T(8,128)}, f32[1,64]{1,0:T(1,128)}) custom-call(f32[8,24,128]{2,1,0:T(8,128)S(1)} %all-to-all-done.3.parts, f32[1,128]{1,0:T(1,128)S(1)} %pad_bitcast_fusion.alpha), custom_call_target="tpu_custom_call" | custom-call | flops 1000000 | bytes 115456 | tf_op jit(solution)/shard_map/newton_step/pallas_call | solution.py:24
  (5 shorter events, 0.0 us)
Async XLA Ops:
  0.6 22.9 %copy-start = (s32[8,256]{1,0:T(8,128)S(1)}, s32[8,256]{1,0:T(8,128)}, u32[]{:S(2)}) copy-start(s32[8,256]{1,0:T(8,128)} %param.10) | copy-start | bytes 24580
  0.6 0.8 copy-start.1
  1.5 0.7 copy-start.3
  2.2 7.9 %collective-permute-start = (f32[6,8,256]{2,1,0:T(8,128)S(1)}, f32[6,8,256]{2,1,0:T(8,128)S(1)}, u32[]{:S(2)}, u32[]{:S(2)}) collective-permute-start(f32[6,8,256]{2,1,0:T(8,128)S(1)} %get-tuple-element.12.up), channel_id=1, source_target_pairs={{0,8},{8,16},{16,24},{24,32},{32,40},{40,48},{48,56},{56,64},{64,7... | collective-permute-start | bytes 147464 | tf_op jit(solution)/shard_map/ppermute | solution.py:260
  7.5 7.5 %collective-permute-start.1 = (f32[6,8,256]{2,1,0:T(8,128)S(1)}, f32[6,8,256]{2,1,0:T(8,128)S(1)}, u32[]{:S(2)}, u32[]{:S(2)}) collective-permute-start(f32[6,8,256]{2,1,0:T(8,128)S(1)} %get-tuple-element.13.down), channel_id=1, source_target_pairs={{8,0},{16,8},{24,16},{32,24},{40,32},{48,40},{56,48},{64,56},{72,6... | collective-permute-start | bytes 147464 | tf_op jit(solution)/shard_map/ppermute | solution.py:261
  16.1 7.5 %copy-start.4 = (f32[64]{0:T(128)S(1)}, f32[64]{0:T(128)}, u32[]{:S(2)}) copy-start(f32[64]{0:T(128)} %param.12) | copy-start | bytes 772
  16.1 13.5 %all-to-all-start = ((f32[8,8,256]{2,1,0:T(8,128)}), f32[8,8,256]{2,1,0:T(8,128)S(1)}, u32[]{:S(2)}, u32[]{:S(2)}) async-start(f32[8,8,256]{2,1,0:T(8,128)} %tangent.1), calls=%async_computation | async-start | bytes 131072 | tf_op jit(solution)/shard_map/all_to_all | solution.py:273
  23.5 0.8 copy-start.2
  30.6 11.6 %all-to-all-start.1 = ((f32[16,24,128]{2,1,0:T(8,128)}), f32[16,24,128]{2,1,0:T(8,128)S(1)}, u32[]{:S(2)}, u32[]{:S(2)}) async-start(f32[16,24,128]{2,1,0:T(8,128)} %gram_block.1), calls=%async_computation.1 | async-start | bytes 393216 | tf_op jit(solution)/shard_map/all_to_all | solution.py:277
  53.6 33.7 %all-to-all-start.3 = ((f32[8,24,128]{2,1,0:T(8,128)}), f32[8,24,128]{2,1,0:T(8,128)S(1)}, u32[]{:S(2)}, u32[]{:S(2)}) async-start(f32[8,24,128]{2,1,0:T(8,128)} %next_sum.1), calls=%async_computation.3 | async-start | bytes 196608 | tf_op jit(solution)/shard_map/all_to_all | solution.py:289
  69.6 11.3 %collective-permute-start.2 = (f32[4,8,256]{2,1,0:T(8,128)S(1)}, f32[4,8,256]{2,1,0:T(8,128)S(1)}, u32[]{:S(2)}, u32[]{:S(2)}) collective-permute-start(f32[4,8,256]{2,1,0:T(8,128)S(1)} %get-tuple-element.19.pup), channel_id=1, source_target_pairs={{0,8},{8,16},{16,24},{24,32},{32,40},{40,48},{48,56},{56,64},{64,7... | collective-permute-start | bytes 98312 | tf_op jit(solution)/shard_map/ppermute | solution.py:286
  78.9 7.3 %collective-permute-start.3 = (f32[4,8,256]{2,1,0:T(8,128)S(1)}, f32[4,8,256]{2,1,0:T(8,128)S(1)}, u32[]{:S(2)}, u32[]{:S(2)}) collective-permute-start(f32[4,8,256]{2,1,0:T(8,128)S(1)} %get-tuple-element.20.pdown), channel_id=1, source_target_pairs={{8,0},{16,8},{24,16},{32,24},{40,32},{48,40},{56,48},{64,56},{72,6... | collective-permute-start | bytes 98312 | tf_op jit(solution)/shard_map/ppermute | solution.py:287

commit v2 on v1

v2 whole, which is shorter than its diff:
```python
import functools

import jax
import jax.numpy as jnp
from jax import lax
from jax.experimental import pallas as pl
from jax.experimental.pallas import tpu as pltpu
from jax.sharding import Mesh
from jax.sharding import PartitionSpec as P

STEPS = 4
F32 = jnp.float32
HI = lax.Precision.HIGHEST
GRID = ("z", "x", "core")
PACK = 24


def vmem():
    return pl.BlockSpec(memory_space=pltpu.VMEM)


def call(body, outs, *args, flops=1_000_000, space=pltpu.VMEM, scratch=()):
    moved = sum(a.size * 4 for a in args) + sum(o.size * 4 for o in outs)
    return pl.pallas_call(
        body,
        out_shape=outs,
        in_specs=[pl.BlockSpec(memory_space=space) for _ in args],
        out_specs=[vmem() for _ in outs],
        scratch_shapes=scratch,
        cost_estimate=pl.CostEstimate(flops=flops, bytes_accessed=moved, transcendentals=0),
        compiler_params=pltpu.CompilerParams(vmem_limit_bytes=8 * 2**20),
        name=body.__name__,
    )(*args)


def shape(*dims):
    return jax.ShapeDtypeStruct(dims, F32)


def iota2(dims, axis):
    return lax.broadcasted_iota(jnp.int32, dims, axis)


def pack_block(field, winds, col, innov, mask, out, *scratch):
    held, sems = scratch[:5], scratch[5]
    copies = [
        pltpu.make_async_copy(source, target, sems.at[n])
        for n, (source, target) in enumerate(zip((field, winds, col, innov, mask), held))
    ]
    for copy in copies:
        copy.start()
    for copy in copies:
        copy.wait()
    out[0:8] = jnp.swapaxes(held[0][...], 0, 1)
    out[8] = held[1][0:8, :]
    out[9] = held[1][8:16, :]
    out[10] = held[2][...].astype(F32)
    out[11] = held[3][...]
    out[12] = jnp.ones((8, 256), F32)
    for m in range(8):
        out[12, :, 8 * m : 8 * m + 8] = held[4][m].astype(F32)


def bin_observations(low, own, high, mine, binned, spread):
    sub = iota2((8, 256), 0)
    chosen = sub == mine[...]
    hits, rows = iota2((256, 256), 0).astype(F32), []
    for kind in range(2):
        picked = []
        for tile in (10, 11):
            if kind == 0:
                source = own[tile]
            else:
                source = jnp.where(
                    sub < 4, pltpu.roll(low[tile], 4, 0), pltpu.roll(high[tile], 4, 0)
                )
            picked.append(jnp.sum(jnp.where(chosen, source, 0.0), axis=0, keepdims=True))
        hit = (hits == picked[0]).astype(F32)
        values = jnp.where(sub == 0, 1.0, jnp.broadcast_to(picked[1], (8, 256)))
        rows.append(
            lax.dot_general(
                values, hit, (((1,), (1,)), ((), ())), precision=HI, preferred_element_type=F32
            )
        )
    binned[...] = jnp.where(sub < 2, rows[0], pltpu.roll(rows[1], 2, 0))
    masks = jnp.concatenate([b[12][:, 0:128] for b in (low, own, high)], axis=0)
    wide = []
    for m in range(8):
        expand = (iota2((128, 256), 0) == 8 * m + iota2((128, 256), 1) // 32).astype(F32)
        wide.append(jnp.dot(masks, expand, preferred_element_type=F32))
    for block in range(4):
        part = jnp.stack([w[8 * (block // 2 + block % 2) : 8 * (block // 2 + block % 2) + 8] for w in wide])
        turned = jnp.swapaxes(part, 0, 1)
        if block == 0:
            spread[0:4] = turned[4:8]
        elif block == 1:
            spread[4:12] = turned
        elif block == 3:
            spread[12:16] = turned[0:4]


def east(x):
    return pltpu.roll(x, 255, 1)


def west(x):
    return pltpu.roll(x, 1, 1)


def wind_rows(blocks, r):
    u = jnp.broadcast_to(blocks[r // 8][8, r % 8 : r % 8 + 1, :], (8, 256))
    v = jnp.broadcast_to(blocks[r // 8][9, r % 8 : r % 8 + 1, :], (8, 256))
    return 0.5 * u, 0.5 * v


def inside(block):
    flag = block[12][:, 128:256]
    return jnp.concatenate([flag, flag], axis=1)


def tangent(low, own, high, kappa, out):
    blocks = (low, own, high)
    k = jnp.broadcast_to(kappa[...], (8, 256))
    below, above = inside(low), inside(high)
    rows = [blocks[r // 8][r % 8] for r in range(24)]
    winds = [wind_rows(blocks, r) for r in range(24)]
    for step in range(1, STEPS + 1):
        new = list(rows)
        for r in range(step, 24 - step):
            hu, hv = winds[r]
            c = rows[r]
            value = (
                (1.0 - 4.0 * k) * c
                + (k - hu) * east(c)
                + (k + hu) * west(c)
                + (k - hv) * rows[r + 1]
                + (k + hv) * rows[r - 1]
            )
            if r < 8:
                value = value * below
            if r > 15:
                value = value * above
            new[r] = value
        rows = new
    for y in range(8):
        out[y, 0] = rows[8 + y]
        out[y, 1] = rows[4 + y] if y < 4 else rows[12 + y]


def adjoint(low, own, high, state, kappa, out):
    blocks = (low, own, high)
    k = jnp.broadcast_to(kappa[...], (8, 256))
    below, above = inside(low), inside(high)
    rows = {4 + e: state[e] for e in range(16)}
    winds = {r: wind_rows(blocks, r) for r in range(4, 20)}
    for step in range(1, STEPS + 1):
        new = dict(rows)
        for r in range(4 + step, 20 - step):
            hu, _ = winds[r]
            c = rows[r]
            value = (
                (1.0 - 4.0 * k) * c
                + east((k + hu) * c)
                + west((k - hu) * c)
                + (k + winds[r + 1][1]) * rows[r + 1]
                + (k - winds[r - 1][1]) * rows[r - 1]
            )
            if r < 8:
                value = value * below
            if r > 15:
                value = value * above
            new[r] = value
        rows = new
    out[...] = jnp.swapaxes(jnp.stack([rows[8 + y] for y in range(8)], axis=0), 0, 1)


def gram_block(field, binned, alpha, out):
    copies = out.shape[0]
    x = field[:, 0].reshape(64, 256)
    ghost = field[:, 1].reshape(64, 256)
    count = binned[0:1, :]
    weighted = jnp.sum(alpha[...] * x, axis=0, keepdims=True) * 0.125
    forcing = binned[1:2, :] - count * weighted
    beyond = jnp.sum(alpha[...] * ghost, axis=0, keepdims=True) * 0.125
    beyond = binned[3:4, :] - binned[2:3, :] * beyond
    left = jnp.concatenate([x * count, jnp.broadcast_to(forcing, (8, 256))], axis=0)
    right = jnp.concatenate([x, x], axis=0)
    g = lax.dot_general(
        left, right, (((1,), (1,)), ((), ())), precision=HI, preferred_element_type=F32
    )
    lane = iota2((16, 128), 1)
    first = lane < 64
    i = iota2((16, 128), 0) + jnp.where(first, 0, 16)
    j = lane % 64
    shifted = pltpu.roll(g[32:64], 96, 1)
    top = jnp.where(first, g[0:16], g[16:32])
    low = jnp.where(first, shifted[0:16], shifted[16:32])
    packed = jnp.where((j < 32) & (i > j), low, top)
    on_diagonal = iota2((32, 128), 1) == iota2((32, 128), 0) + 96
    diagonal = jnp.sum(jnp.where(on_diagonal, g[32:64], 0.0), axis=0, keepdims=True)
    sub = iota2((8, 128), 0)
    extra = jnp.where(iota2((8, 128), 1) < 64, g[64:72], diagonal)
    tail = extra
    for n, line in enumerate((forcing, beyond)):
        for h in range(2):
            tail = jnp.where(sub == 2 * n + h + 1, line[:, 128 * h : 128 * h + 128], tail)
    for c in range(copies):
        out[c, 0:16, :] = packed
        out[c, 16:24, :] = tail


def sum_blocks(parts):
    total = parts[0]
    for c in range(1, parts.shape[0]):
        total = total + parts[c]
    return total


def first_sum(parts, spread, core, out, state):
    rows = parts.shape[0] // 2
    total = parts[0:PACK, :]
    for c in range(1, parts.shape[0] // PACK):
        total = total + parts[PACK * c : PACK * c + PACK, :]
    for c in range(out.shape[0]):
        out[c] = total
    odd = core[...] > 0.5
    forcing = []
    for n in range(2):
        halves = []
        for h in range(2):
            a = parts[pl.ds(17 + 2 * n + h, 8, stride=PACK), :]
            b = parts[pl.ds(17 + 2 * n + h + rows, 8, stride=PACK), :]
            halves.append(jnp.where(odd, b, a))
        forcing.append(jnp.concatenate(halves, axis=1))
    for e in range(16):
        if e < 4:
            line = forcing[1][e : e + 1, :]
        elif e < 12:
            line = forcing[0][e - 4 : e - 3, :]
        else:
            line = forcing[1][e - 8 : e - 7, :]
        state[e] = spread[e] * line


def next_sum(parts, out):
    total = sum_blocks(parts)
    for c in range(out.shape[0]):
        out[c] = total


def across(tile, lane):
    return jnp.broadcast_to(tile[:, lane : lane + 1], tile.shape)


def along(tile, row):
    return jnp.broadcast_to(tile[row : row + 1, :], tile.shape)


def newton_step(count, parts, alpha, factor, newton):
    total = sum_blocks(parts)
    packed, extra = total[0:16], total[16:17]
    lane, sub = iota2((32, 128), 1), iota2((32, 128), 0)
    s = jnp.concatenate([packed, pltpu.roll(packed, 64, 1)], axis=0)
    top = jnp.where((lane >= sub) & (lane < 64), s, 0.0)
    diagonal = pltpu.roll(jnp.broadcast_to(extra, (32, 128)), 64, 1)
    bottom = jnp.where(
        lane == sub + 32,
        diagonal,
        jnp.where((lane >= 32) & (lane < sub + 32), pltpu.roll(s, 32, 1), 0.0),
    )
    scale = 1.0 / count
    rhs = alpha[...] - 8.0 * extra * scale
    rest = jnp.where(iota2((64, 128), 0) == 0, jnp.broadcast_to(rhs, (64, 128)), 0.0)
    z = jnp.concatenate([top, bottom, rest], axis=0)
    turned = jnp.transpose(z)[0:64]
    lanes, subs = iota2((64, 128), 1), iota2((64, 128), 0)
    both = z[0:64] + jnp.where((lanes == subs) | (lanes >= 64), 0.0, turned)
    a = jnp.where((lanes == subs) | (lanes == subs + 64), 1.0, 0.0) + both * scale
    tiles = [a[8 * t : 8 * t + 8] for t in range(8)]
    right = [across(turned[8 * t : 8 * t + 8], 64) for t in range(8)]
    lane1 = iota2((1, 128), 1)
    solved = jnp.zeros((8, 128), F32)
    for t in range(8):
        base = 8 * t
        columns = [across(tiles[t], base + c) for c in range(8)]
        e = {(i, c): along(columns[c], i) for c in range(8) for i in range(c, 8)}
        line = [along(tiles[t], q) for q in range(8)]
        b = [along(right[t], q) for q in range(8)]
        low, inverse = {}, []
        for c in range(8):
            inverse.append(1.0 / e[c, c])
            for i in range(c + 1, 8):
                low[i, c] = e[i, c] * inverse[c]
            for j in range(c + 1, 8):
                for i in range(j, 8):
                    e[i, j] = e[i, j] - low[i, c] * e[j, c]
            for i in range(c + 1, 8):
                line[i] = line[i] - low[i, c] * line[c]
                b[i] = b[i] - low[i, c] * b[c]
        for i in range(t + 1, 8):
            c_of = []
            for c in range(8):
                value = across(tiles[i], base + c)
                for j in range(c):
                    value = value - c_of[j] * low[c, j]
                c_of.append(value)
            for c in range(8):
                mult = c_of[c] * inverse[c]
                tiles[i] = tiles[i] - mult * line[c]
                right[i] = right[i] - mult * b[c]
        for q in range(8):
            solved = solved + line[q] * (b[q] * inverse[q])
            upper = line[q][0:1] * lax.rsqrt(e[q, q][0:1])
            upper = jnp.where(lane1 >= base + q, upper, 0.0)
            factor[base + q : base + q + 1, :] = upper[:, 0:64]
    newton[...] = pltpu.roll(solved, 64, 1)[0:1, 0:64]


def per_device(perturb, winds, kappa, obs_col, innov, alpha, loc_mask):
    ny = lax.axis_size("y")
    blocks = lax.axis_size(GRID)
    count = float(blocks * 8 * 256)
    sources = (
        perturb.reshape(8, 8, 256),
        winds.reshape(16, 256),
        obs_col,
        innov.reshape(8, 256),
        loc_mask,
    )
    (own,) = call(
        pack_block,
        [shape(13, 8, 256)],
        *(pltpu.with_memory_space_constraint(a, pltpu.HBM) for a in sources),
        space=pltpu.HBM,
        scratch=[pltpu.VMEM(a.shape, a.dtype) for a in sources]
        + [pltpu.SemaphoreType.DMA((len(sources),))],
    )
    low = lax.ppermute(own, GRID, [(i, i + 1) for i in range(blocks - 1)])
    high = lax.ppermute(own, GRID, [(i + 1, i) for i in range(blocks - 1)])
    core = lax.axis_index("core").astype(F32).reshape(1, 1)
    k = kappa.reshape(1, 1)
    (evolved,) = call(tangent, [shape(8, 2, 8, 256)], low, own, high, k)
    binned, spread = call(
        bin_observations,
        [shape(8, 256), shape(16, 8, 256)],
        low,
        own,
        high,
        lax.axis_index("y").reshape(1, 1),
    )
    field = lax.all_to_all(evolved, "y", 0, 0, tiled=True)
    (part,) = call(
        gram_block, [shape(2 * ny, PACK, 128)], field, binned, alpha.reshape(64, 1)
    )
    parts = lax.all_to_all(part, ("core", "y"), 0, 0, tiled=True)
    part, state = call(
        first_sum,
        [shape(lax.axis_size("x"), PACK, 128), shape(16, 8, 256)],
        parts.reshape(-1, 128),
        spread,
        core,
    )
    parts = lax.all_to_all(part, "x", 0, 0, tiled=True)
    (part,) = call(next_sum, [shape(lax.axis_size("z"), PACK, 128)], parts)
    parts = lax.all_to_all(part, "z", 0, 0, tiled=True)
    (sens,) = call(adjoint, [shape(8, 8, 256)], low, own, high, state, k)
    wide = jnp.concatenate([alpha, jnp.zeros((64,), F32)]).reshape(1, 128)
    final = functools.partial(newton_step, count)
    final.__name__ = "newton_step"
    factor, newton = call(final, [shape(64, 64), shape(1, 64)], parts, wide)
    return factor, newton.reshape(64), sens.reshape(8, 1, 8, 256)


def solution(mesh):
    grid, mem = mesh.devices.shape
    side = int((grid // 2) ** 0.5)
    fine = Mesh(mesh.devices.reshape(side, grid // 2 // side, 2, mem), GRID + ("y",))
    in_specs = (
        P("y", None, GRID, None),
        P(None, None, GRID, None),
        P(),
        P(GRID, None),
        P(None, GRID, None),
        P(),
        P("y", GRID, None),
    )
    out_specs = (P(), P(), P("y", None, GRID, None))
    return jax.shard_map(
        per_device, mesh=fine, in_specs=in_specs, out_specs=out_specs, check_vma=False
    )
```

time: 97.3 us -> 87.5 us (0.90)
  the two profiles are of different devices: /device:TPU:31 before, /device:TPU:16 now
where the time goes in v2:
time: 87.5 us; the launch traced here: 86.9 us
  starting transfers between devices  38.8 us (44%)
  waiting for transfers between devices  26.5 us (30%)
  blocking collectives  11.1 us (13%)
  Pallas kernels  8.42 us (10%)
  between operations  1.33 us (2%)
    all_to_all x1, starting transfers between devices, per_device(): parts = lax.all_to_all(part, 'z', 0, 0, tiled=True)  16.5 us
    all_to_all x1, starting transfers between devices, per_device(): field = lax.all_to_all(evolved, 'y', 0, 0, tiled=True)  14.5 us
    all_to_all x1, blocking collectives, per_device(): parts = lax.all_to_all(part, 'x', 0, 0, tiled=True)  11.1 us
    all_to_all x1, waiting for transfers between devices, per_device(): parts = lax.all_to_all(part, ('core', 'y'), 0, 0, tiled=True)  9.64 us
    pallas_call x8, Pallas kernels, call(): pl.pallas_call(body, out_shape=outs, in_specs=[pl.BlockSpec(memory_space=...  8.42 us
    all_to_all x1, waiting for transfers between devices, per_device(): parts = lax.all_to_all(part, 'z', 0, 0, tiled=True)  7.62 us
    all_to_all x1, waiting for transfers between devices, per_device(): field = lax.all_to_all(evolved, 'y', 0, 0, tiled=True)  6.69 us
    all_to_all x1, starting transfers between devices, per_device(): parts = lax.all_to_all(part, ('core', 'y'), 0, 0, tiled=True)  4.82 us
  transfers between devices with their start and end apart: 5, of which 4 were waited for; matrix products, arithmetic and copies ran while one was open for 0% of the time, Pallas kernels for 2%

profile of v2, /device:TPU:16, one launch (start us, length us, event | category | flops | bytes accessed | tf_op | source)
XLA Modules:
  0.0 86.9 jit_solution(9249856182264713012)
XLA Ops:
  0.6 1.0 %pack_block.1.own = f32[13,8,256]{2,1,0:T(8,128)S(1)} custom-call(f32[8,8,256]{2,1,0:T(8,128)} %bitcast.18, f32[16,256]{1,0:T(8,128)} %bitcast.19, s32[8,256]{1,0:T(8,128)} %col.1, f32[8,256]{1,0:T(8,128)} %bitcast.20, s32[8,8,8]{2,1,0:T(8,128)} %mask.1), custom_call_target="tpu_custom_call" | custom-call | flops 1000000 | bytes 206848 | tf_op jit(solution)/shard_map/pack_block/pallas_call | solution.py:24
  1.6 1.7 %collective-permute-start = (f32[13,8,256]{2,1,0:T(8,128)S(1)}, f32[13,8,256]{2,1,0:T(8,128)S(1)}, u32[]{:S(2)}, u32[]{:S(2)}) collective-permute-start(f32[13,8,256]{2,1,0:T(8,128)S(1)} %pack_block.1.own), channel_id=1, source_target_pairs={{0,8},{8,16},{16,24},{24,32},{32,40},{40,48},{48,56},{56,64},{64,7... | collective-permute-start | bytes 319496 | tf_op jit(solution)/shard_map/ppermute | solution.py:338
  3.4 1.3 %collective-permute-start.1 = (f32[13,8,256]{2,1,0:T(8,128)S(1)}, f32[13,8,256]{2,1,0:T(8,128)S(1)}, u32[]{:S(2)}, u32[]{:S(2)}) collective-permute-start(f32[13,8,256]{2,1,0:T(8,128)S(1)} %pack_block.1.own), channel_id=1, source_target_pairs={{8,0},{16,8},{24,16},{32,24},{40,32},{48,40},{56,48},{64,56},{72,6... | collective-permute-start | bytes 319496 | tf_op jit(solution)/shard_map/ppermute | solution.py:339
  5.3 0.0 collective-permute-done.low
  5.3 2.5 %collective-permute-done.1.high = f32[13,8,256]{2,1,0:T(8,128)S(1)} collective-permute-done((f32[13,8,256]{2,1,0:T(8,128)S(1)}, f32[13,8,256]{2,1,0:T(8,128)S(1)}, u32[]{:S(2)}, u32[]{:S(2)}) %collective-permute-start.1) | collective-permute-done | bytes 106528 | tf_op jit(solution)/shard_map/ppermute | solution.py:339
  7.8 1.1 %tangent.1 = f32[8,2,8,256]{3,2,1,0:T(8,128)} custom-call(f32[13,8,256]{2,1,0:T(8,128)S(1)} %collective-permute-done.low, f32[13,8,256]{2,1,0:T(8,128)S(1)} %pack_block.1.own, f32[13,8,256]{2,1,0:T(8,128)S(1)} %collective-permute-done.1.high, f32[1,1]{1,0:T(1,128)} %bitcast.14.kappa), custom_call_target="tpu_custom_call" | custom-call | flops 1000000 | bytes 450564 | tf_op jit(solution)/shard_map/tangent/pallas_call | solution.py:24
  8.9 14.5 %all-to-all-start = ((f32[8,2,8,256]{3,2,1,0:T(8,128)}), f32[8,2,8,256]{3,2,1,0:T(8,128)S(1)}, u32[]{:S(2)}, u32[]{:S(2)}) async-start(f32[8,2,8,256]{3,2,1,0:T(8,128)} %tangent.1), calls=%async_computation | async-start | bytes 262144 | tf_op jit(solution)/shard_map/all_to_all | solution.py:351
  23.5 0.0 copy-start
  23.5 0.7 copy-done
  24.1 0.1 copy.10.alpha
  24.2 0.7 bin_observations.1
  24.9 6.7 %all-to-all-done.field = f32[8,2,8,256]{3,2,1,0:T(8,128)S(1)} async-done(((f32[8,2,8,256]{3,2,1,0:T(8,128)}), f32[8,2,8,256]{3,2,1,0:T(8,128)S(1)}, u32[]{:S(2)}, u32[]{:S(2)}) %all-to-all-start) | async-done | bytes 131104 | tf_op jit(solution)/shard_map/all_to_all | solution.py:351
  31.6 1.0 %gram_block.1 = f32[16,24,128]{2,1,0:T(8,128)} custom-call(f32[8,2,8,256]{3,2,1,0:T(8,128)S(1)} %all-to-all-done.field, f32[8,256]{1,0:T(8,128)S(1)} %get-tuple-element.9.binned, f32[64,1]{1,0:T(8,128)S(1)} %copy.10.alpha), custom_call_target="tpu_custom_call" | custom-call | flops 1000000 | bytes 336128 | tf_op jit(solution)/shard_map/gram_block/pallas_call | solution.py:24
  32.7 4.8 %all-to-all-start.1 = ((f32[16,24,128]{2,1,0:T(8,128)}), f32[16,24,128]{2,1,0:T(8,128)S(1)}, u32[]{:S(2)}, u32[]{:S(2)}) async-start(f32[16,24,128]{2,1,0:T(8,128)} %gram_block.1), calls=%async_computation.1 | async-start | bytes 393216 | tf_op jit(solution)/shard_map/all_to_all | solution.py:355
  37.5 9.6 %all-to-all-done.1 = f32[16,24,128]{2,1,0:T(8,128)S(1)} async-done(((f32[16,24,128]{2,1,0:T(8,128)}), f32[16,24,128]{2,1,0:T(8,128)S(1)}, u32[]{:S(2)}, u32[]{:S(2)}) %all-to-all-start.1) | async-done | bytes 196640 | tf_op jit(solution)/shard_map/all_to_all | solution.py:355
  47.1 0.1 first_sum.1
  47.2 11.1 %all_to_all.20.parts = f32[8,24,128]{2,1,0:T(8,128)S(1)} all-to-all(f32[8,24,128]{2,1,0:T(8,128)S(1)} %get-tuple-element.11), channel_id=1, replica_groups=mesh['z'=8,'x'=8,'core'=2,'y'=8] {'x'}, dimensions={0} | all-to-all | bytes 196608 | tf_op jit(solution)/shard_map/all_to_all | solution.py:363
  58.3 0.6 next_sum.1
  59.0 16.5 %all-to-all-start.3 = ((f32[8,24,128]{2,1,0:T(8,128)}), f32[8,24,128]{2,1,0:T(8,128)S(1)}, u32[]{:S(2)}, u32[]{:S(2)}) async-start(f32[8,24,128]{2,1,0:T(8,128)} %next_sum.1), calls=%async_computation.3 | async-start | bytes 196608 | tf_op jit(solution)/shard_map/all_to_all | solution.py:365
  75.4 1.1 %adjoint.1 = f32[8,8,256]{2,1,0:T(8,128)} custom-call(f32[13,8,256]{2,1,0:T(8,128)S(1)} %collective-permute-done.low, f32[13,8,256]{2,1,0:T(8,128)S(1)} %pack_block.1.own, f32[13,8,256]{2,1,0:T(8,128)S(1)} %collective-permute-done.1.high, f32[16,8,256]{2,1,0:T(8,128)S(1)} %get-tuple-element.14.state, f32[1,1]{1,0:T(1,128)} %bitcast.15.kappa), custom_call_target="tpu_custom_call" | custom-call | flops 1000000 | bytes 516100 | tf_op jit(solution)/shard_map/adjoint/pallas_call | solution.py:24
  76.5 7.6 %all-to-all-done.3.parts = f32[8,24,128]{2,1,0:T(8,128)S(1)} async-done(((f32[8,24,128]{2,1,0:T(8,128)}), f32[8,24,128]{2,1,0:T(8,128)S(1)}, u32[]{:S(2)}, u32[]{:S(2)}) %all-to-all-start.3) | async-done | bytes 98336 | tf_op jit(solution)/shard_map/all_to_all | solution.py:365
  84.2 2.8 %newton_step.1 = (f32[64,64]{1,0:T(8,128)}, f32[1,64]{1,0:T(1,128)}) custom-call(f32[8,24,128]{2,1,0:T(8,128)S(1)} %all-to-all-done.3.parts, f32[1,128]{1,0:T(1,128)S(1)} %pad_bitcast_fusion.alpha), custom_call_target="tpu_custom_call" | custom-call | flops 1000000 | bytes 115456 | tf_op jit(solution)/shard_map/newton_step/pallas_call | solution.py:24
  (1 shorter events, 0.0 us)
Async XLA Ops:
  1.6 3.7 %collective-permute-start = (f32[13,8,256]{2,1,0:T(8,128)S(1)}, f32[13,8,256]{2,1,0:T(8,128)S(1)}, u32[]{:S(2)}, u32[]{:S(2)}) collective-permute-start(f32[13,8,256]{2,1,0:T(8,128)S(1)} %pack_block.1.own), channel_id=1, source_target_pairs={{0,8},{8,16},{16,24},{24,32},{32,40},{40,48},{48,56},{56,64},{64,7... | collective-permute-start | bytes 319496 | tf_op jit(solution)/shard_map/ppermute | solution.py:338
  3.4 4.5 %collective-permute-start.1 = (f32[13,8,256]{2,1,0:T(8,128)S(1)}, f32[13,8,256]{2,1,0:T(8,128)S(1)}, u32[]{:S(2)}, u32[]{:S(2)}) collective-permute-start(f32[13,8,256]{2,1,0:T(8,128)S(1)} %pack_block.1.own), channel_id=1, source_target_pairs={{8,0},{16,8},{24,16},{32,24},{40,32},{48,40},{56,48},{64,56},{72,6... | collective-permute-start | bytes 319496 | tf_op jit(solution)/shard_map/ppermute | solution.py:339
  8.9 22.7 %all-to-all-start = ((f32[8,2,8,256]{3,2,1,0:T(8,128)}), f32[8,2,8,256]{3,2,1,0:T(8,128)S(1)}, u32[]{:S(2)}, u32[]{:S(2)}) async-start(f32[8,2,8,256]{3,2,1,0:T(8,128)} %tangent.1), calls=%async_computation | async-start | bytes 262144 | tf_op jit(solution)/shard_map/all_to_all | solution.py:351
  23.5 0.7 copy-start
  32.7 14.5 %all-to-all-start.1 = ((f32[16,24,128]{2,1,0:T(8,128)}), f32[16,24,128]{2,1,0:T(8,128)S(1)}, u32[]{:S(2)}, u32[]{:S(2)}) async-start(f32[16,24,128]{2,1,0:T(8,128)} %gram_block.1), calls=%async_computation.1 | async-start | bytes 393216 | tf_op jit(solution)/shard_map/all_to_all | solution.py:355
  59.0 25.2 %all-to-all-start.3 = ((f32[8,24,128]{2,1,0:T(8,128)}), f32[8,24,128]{2,1,0:T(8,128)S(1)}, u32[]{:S(2)}, u32[]{:S(2)}) async-start(f32[8,24,128]{2,1,0:T(8,128)} %next_sum.1), calls=%async_computation.3 | async-start | bytes 196608 | tf_op jit(solution)/shard_map/all_to_all | solution.py:365

commit v3 on v2

--- a/solution.py
+++ b/solution.py
@@ -56,106 +56,92 @@
     out[9] = held[1][8:16, :]
     out[10] = held[2][...].astype(F32)
     out[11] = held[3][...]
-    out[12] = jnp.ones((8, 256), F32)
+    out[12] = jnp.zeros((8, 256), F32)
     for m in range(8):
         out[12, :, 8 * m : 8 * m + 8] = held[4][m].astype(F32)
 
 
-def bin_observations(low, own, high, mine, binned, spread):
+def east(x):
+    return pltpu.roll(x, 255, 1)
+
+
+def west(x):
+    return pltpu.roll(x, 1, 1)
+
+
+def wind_rows(blocks, r):
+    u = jnp.broadcast_to(blocks[r // 8][8, r % 8 : r % 8 + 1, :], (8, 256))
+    v = jnp.broadcast_to(blocks[r // 8][9, r % 8 : r % 8 + 1, :], (8, 256))
+    return 0.5 * u, 0.5 * v
+
+
+def select_row(tile, sub, mine):
+    return jnp.sum(jnp.where(sub == mine, tile, 0.0), axis=0, keepdims=True)
+
+
+def tangent(low, own, kappa, mine, joined, alpha, core, follows, out, binned, column_of):
+    column_of[...] = jnp.transpose(jnp.broadcast_to(alpha[...], (128, 128)))[0:64]
+    blocks = (low, own)
+    k = jnp.broadcast_to(kappa[...], (8, 256))
+    joint = jnp.broadcast_to(joined[...], (8, 256))
+    rows = [blocks[r // 8][r % 8] for r in range(16)]
+    winds = [wind_rows(blocks, r) for r in range(16)]
+    for step in range(1, STEPS + 1):
+        new = list(rows)
+        for r in range(step, 16 - step):
+            hu, hv = winds[r]
+            c = rows[r]
+            north = (k - hv) * rows[r + 1]
+            south = (k + hv) * rows[r - 1]
+            if r == 7:
+                north = north * joint
+            if r == 8:
+                south = south * joint
+            new[r] = (
+                (1.0 - 4.0 * k) * c + (k - hu) * east(c) + (k + hu) * west(c) + north + south
+            )
+        rows = new
+    for y in range(8):
+        out[y] = rows[4 + y]
     sub = iota2((8, 256), 0)
-    chosen = sub == mine[...]
-    hits, rows = iota2((256, 256), 0).astype(F32), []
-    for kind in range(2):
-        picked = []
-        for tile in (10, 11):
-            if kind == 0:
-                source = own[tile]
-            else:
-                source = jnp.where(
-                    sub < 4, pltpu.roll(low[tile], 4, 0), pltpu.roll(high[tile], 4, 0)
-                )
-            picked.append(jnp.sum(jnp.where(chosen, source, 0.0), axis=0, keepdims=True))
-        hit = (hits == picked[0]).astype(F32)
-        values = jnp.where(sub == 0, 1.0, jnp.broadcast_to(picked[1], (8, 256)))
-        rows.append(
-            lax.dot_general(
-                values, hit, (((1,), (1,)), ((), ())), precision=HI, preferred_element_type=F32
-            )
-        )
-    binned[...] = jnp.where(sub < 2, rows[0], pltpu.roll(rows[1], 2, 0))
-    masks = jnp.concatenate([b[12][:, 0:128] for b in (low, own, high)], axis=0)
+    turned = [
+        jnp.where(sub < 4, pltpu.roll(low[tile], 4, 0), pltpu.roll(own[tile], 4, 0))
+        for tile in (10, 11)
+    ]
+    column, value = (select_row(tile, sub, mine[...]) for tile in turned)
+    hit = (iota2((256, 256), 0).astype(F32) == column).astype(F32)
+    values = jnp.where(sub == 0, 1.0, jnp.broadcast_to(value, (8, 256)))
+    binned[...] = lax.dot_general(
+        values, hit, (((1,), (1,)), ((), ())), precision=HI, preferred_element_type=F32
+    )
+
+
+def adjoint(low, own, window, beyond, kappa, joined, follows, out):
+    k = jnp.broadcast_to(kappa[...], (8, 256))
+    below = jnp.broadcast_to(joined[...], (8, 256))
+    above = jnp.broadcast_to(follows[...], (8, 256))
+    masks = jnp.concatenate([b[:, 0:128] for b in (low[12], own[12], beyond[3])], axis=0)
     wide = []
     for m in range(8):
         expand = (iota2((128, 256), 0) == 8 * m + iota2((128, 256), 1) // 32).astype(F32)
         wide.append(jnp.dot(masks, expand, preferred_element_type=F32))
-    for block in range(4):
-        part = jnp.stack([w[8 * (block // 2 + block % 2) : 8 * (block // 2 + block % 2) + 8] for w in wide])
-        turned = jnp.swapaxes(part, 0, 1)
-        if block == 0:
-            spread[0:4] = turned[4:8]
-        elif block == 1:
-            spread[4:12] = turned
-        elif block == 3:
-            spread[12:16] = turned[0:4]
-
-
-def east(x):
-    return pltpu.roll(x, 255, 1)
-
-
-def west(x):
-    return pltpu.roll(x, 1, 1)
-
-
-def wind_rows(blocks, r):
-    u = jnp.broadcast_to(blocks[r // 8][8, r % 8 : r % 8 + 1, :], (8, 256))
-    v = jnp.broadcast_to(blocks[r // 8][9, r % 8 : r % 8 + 1, :], (8, 256))
-    return 0.5 * u, 0.5 * v
-
-
-def inside(block):
-    flag = block[12][:, 128:256]
-    return jnp.concatenate([flag, flag], axis=1)
-
-
-def tangent(low, own, high, kappa, out):
-    blocks = (low, own, high)
-    k = jnp.broadcast_to(kappa[...], (8, 256))
-    below, above = inside(low), inside(high)
-    rows = [blocks[r // 8][r % 8] for r in range(24)]
-    winds = [wind_rows(blocks, r) for r in range(24)]
-    for step in range(1, STEPS + 1):
-        new = list(rows)
-        for r in range(step, 24 - step):
-            hu, hv = winds[r]
-            c = rows[r]
-            value = (
-                (1.0 - 4.0 * k) * c
-                + (k - hu) * east(c)
-                + (k + hu) * west(c)
-                + (k - hv) * rows[r + 1]
-                + (k + hv) * rows[r - 1]
-            )
-            if r < 8:
-                value = value * below
-            if r > 15:
-                value = value * above
-            new[r] = value
-        rows = new
-    for y in range(8):
-        out[y, 0] = rows[8 + y]
-        out[y, 1] = rows[4 + y] if y < 4 else rows[12 + y]
-
-
-def adjoint(low, own, high, state, kappa, out):
-    blocks = (low, own, high)
-    k = jnp.broadcast_to(kappa[...], (8, 256))
-    below, above = inside(low), inside(high)
-    rows = {4 + e: state[e] for e in range(16)}
-    winds = {r: wind_rows(blocks, r) for r in range(4, 20)}
+    spread = [
+        jnp.swapaxes(jnp.stack([w[8 * n : 8 * n + 8] for w in wide]), 0, 1) for n in range(3)
+    ]
+    rows, winds = {}, {}
+    for e in range(16):
+        line = window[0, e : e + 1, :] if e < 8 else beyond[0, e - 8 : e - 7, :]
+        n, y = divmod(e + 4, 8)
+        rows[e] = spread[n][y] * line
+        if e < 4:
+            rows[e] = rows[e] * below
+        if e > 11:
+            rows[e] = rows[e] * above
+        u, v = ((low[8], low[9]), (own[8], own[9]), (beyond[1], beyond[2]))[n]
+        winds[e] = tuple(0.5 * jnp.broadcast_to(w[y : y + 1], (8, 256)) for w in (u, v))
     for step in range(1, STEPS + 1):
         new = dict(rows)
-        for r in range(4 + step, 20 - step):
+        for r in range(step, 16 - step):
             hu, _ = winds[r]
             c = rows[r]
             value = (
@@ -165,24 +151,22 @@
                 + (k + winds[r + 1][1]) * rows[r + 1]
                 + (k - winds[r - 1][1]) * rows[r - 1]
             )
-            if r < 8:
+            if r < 4:
                 value = value * below
-            if r > 15:
+            if r > 11:
                 value = value * above
             new[r] = value
         rows = new
-    out[...] = jnp.swapaxes(jnp.stack([rows[8 + y] for y in range(8)], axis=0), 0, 1)
+    out[...] = jnp.swapaxes(jnp.stack([rows[4 + y] for y in range(8)], axis=0), 0, 1)
 
 
 def gram_block(field, binned, alpha, out):
     copies = out.shape[0]
-    x = field[:, 0].reshape(64, 256)
-    ghost = field[:, 1].reshape(64, 256)
+    x = field[...].reshape(64, 256)
     count = binned[0:1, :]
-    weighted = jnp.sum(alpha[...] * x, axis=0, keepdims=True) * 0.125
+    weights = jnp.concatenate([alpha[...], alpha[...]], axis=1)
+    weighted = jnp.sum(weights * x, axis=0, keepdims=True) * 0.125
     forcing = binned[1:2, :] - count * weighted
-    beyond = jnp.sum(alpha[...] * ghost, axis=0, keepdims=True) * 0.125
-    beyond = binned[3:4, :] - binned[2:3, :] * beyond
     left = jnp.concatenate([x * count, jnp.broadcast_to(forcing, (8, 256))], axis=0)
     right = jnp.concatenate([x, x], axis=0)
     g = lax.dot_general(
@@ -201,9 +185,8 @@
     sub = iota2((8, 128), 0)
     extra = jnp.where(iota2((8, 128), 1) < 64, g[64:72], diagonal)
     tail = extra
-    for n, line in enumerate((forcing, beyond)):
-        for h in range(2):
-            tail = jnp.where(sub == 2 * n + h + 1, line[:, 128 * h : 128 * h + 128], tail)
+    for h in range(2):
+        tail = jnp.where(sub == h + 1, forcing[:, 128 * h : 128 * h + 128], tail)
     for c in range(copies):
         out[c, 0:16, :] = packed
         out[c, 16:24, :] = tail
@@ -216,7 +199,7 @@
     return total
 
 
-def first_sum(parts, spread, core, out, state):
+def first_sum(parts, own, core, out, window):
     rows = parts.shape[0] // 2
     total = parts[0:PACK, :]
     for c in range(1, parts.shape[0] // PACK):
@@ -224,22 +207,13 @@
     for c in range(out.shape[0]):
         out[c] = total
     odd = core[...] > 0.5
-    forcing = []
-    for n in range(2):
-        halves = []
-        for h in range(2):
-            a = parts[pl.ds(17 + 2 * n + h, 8, stride=PACK), :]
-            b = parts[pl.ds(17 + 2 * n + h + rows, 8, stride=PACK), :]
-            halves.append(jnp.where(odd, b, a))
-        forcing.append(jnp.concatenate(halves, axis=1))
-    for e in range(16):
-        if e < 4:
-            line = forcing[1][e : e + 1, :]
-        elif e < 12:
-            line = forcing[0][e - 4 : e - 3, :]
-        else:
-            line = forcing[1][e - 8 : e - 7, :]
-        state[e] = spread[e] * line
+    for h in range(2):
+        a = parts[pl.ds(17 + h, 8, stride=PACK), :]
+        b = parts[pl.ds(17 + h + rows, 8, stride=PACK), :]
+        window[0, :, 128 * h : 128 * h + 128] = jnp.where(odd, b, a)
+    window[1] = own[8]
+    window[2] = own[9]
+    window[3] = own[12]
 
 
 def next_sum(parts, out):
@@ -335,36 +309,43 @@
         scratch=[pltpu.VMEM(a.shape, a.dtype) for a in sources]
         + [pltpu.SemaphoreType.DMA((len(sources),))],
     )
-    low = lax.ppermute(own, GRID, [(i, i + 1) for i in range(blocks - 1)])
-    high = lax.ppermute(own, GRID, [(i + 1, i) for i in range(blocks - 1)])
+    low = lax.ppermute(own, GRID, [(i, (i + 1) % blocks) for i in range(blocks)])
+    index = lax.axis_index(GRID)
     core = lax.axis_index("core").astype(F32).reshape(1, 1)
+    joined = (index > 0).astype(F32).reshape(1, 1)
+    follows = (index < blocks - 1).astype(F32).reshape(1, 1)
+    mine = lax.axis_index("y").reshape(1, 1)
     k = kappa.reshape(1, 1)
-    (evolved,) = call(tangent, [shape(8, 2, 8, 256)], low, own, high, k)
-    binned, spread = call(
-        bin_observations,
-        [shape(8, 256), shape(16, 8, 256)],
+    wide = jnp.concatenate([alpha, jnp.zeros((64,), F32)]).reshape(1, 128)
+    evolved, binned, column = call(
+        tangent,
+        [shape(8, 8, 256), shape(8, 256), shape(64, 128)],
         low,
         own,
-        high,
-        lax.axis_index("y").reshape(1, 1),
+        k,
+        mine,
+        joined,
+        wide,
+        core,
+        follows,
     )
     field = lax.all_to_all(evolved, "y", 0, 0, tiled=True)
-    (part,) = call(
-        gram_block, [shape(2 * ny, PACK, 128)], field, binned, alpha.reshape(64, 1)
-    )
+    (part,) = call(gram_block, [shape(2 * ny, PACK, 128)], field, binned, column)
     parts = lax.all_to_all(part, ("core", "y"), 0, 0, tiled=True)
-    part, state = call(
+    part, window = call(
         first_sum,
-        [shape(lax.axis_size("x"), PACK, 128), shape(16, 8, 256)],
+        [shape(lax.axis_size("x"), PACK, 128), shape(4, 8, 256)],
         parts.reshape(-1, 128),
-        spread,
+        own,
         core,
     )
     parts = lax.all_to_all(part, "x", 0, 0, tiled=True)
     (part,) = call(next_sum, [shape(lax.axis_size("z"), PACK, 128)], parts)
     parts = lax.all_to_all(part, "z", 0, 0, tiled=True)
-    (sens,) = call(adjoint, [shape(8, 8, 256)], low, own, high, state, k)
-    wide = jnp.concatenate([alpha, jnp.zeros((64,), F32)]).reshape(1, 128)
+    beyond = lax.ppermute(window, GRID, [((i + 1) % blocks, i) for i in range(blocks)])
+    (sens,) = call(
+        adjoint, [shape(8, 8, 256)], low, own, window, beyond, k, joined, follows
+    )
     final = functools.partial(newton_step, count)
     final.__name__ = "newton_step"
     factor, newton = call(final, [shape(64, 64), shape(1, 64)], parts, wide)

time: 87.5 us -> 82.4 us (0.942)
  starting transfers between devices: 38.8 us -> 10.5 us
  blocking collectives: 11.1 us -> 39.2 us
  waiting for transfers between devices: 26.5 us -> 24.3 us
  Pallas kernels: 8.42 us -> 6.52 us
    all_to_all x0 -> x2, blocking collectives: none -> 28.1 us  [the longest x1 14.6 us: per_device(): field = lax.all_to_all(evolved, 'y', 0, 0, tiled=True)]
    all_to_all x2 -> x0, starting transfers between devices: 19.3 us -> none  [the longest x1 14.5 us: per_device(): field = lax.all_to_all(evolved, 'y', 0, 0, tiled=True)]
    ppermute x2, waiting for transfers between devices: 2.52 us -> 20.4 us  [the longest x1 18.8 us: per_device(): lax.ppermute(own, GRID, [(i, (i + 1) % blocks) for i in range(blocks)])]
    all_to_all x2 -> x0, waiting for transfers between devices: 16.3 us -> none  [the longest x1 9.64 us: per_device(): parts = lax.all_to_all(part, ('core', 'y'), 0, 0, tiled=True)]
    all_to_all x1, starting transfers between devices: 16.5 us -> 6.65 us  [per_device(): parts = lax.all_to_all(part, 'z', 0, 0, tiled=True)]
    all_to_all x1, waiting for transfers between devices: 7.62 us -> 3.97 us  [per_device(): parts = lax.all_to_all(part, 'z', 0, 0, tiled=True)]
    pallas_call x8 -> x7, Pallas kernels: 8.42 us -> 6.52 us  [call(): pl.pallas_call(body, out_shape=outs, in_specs=[pl.BlockSpec(memory_space=...]
  transfers between devices with their start and end apart: 5 -> 3, of which waited for: 4 -> 3; matrix products, arithmetic and copies ran while one was open for 0% -> 0% of each run, Pallas kernels for 2% -> 2%
where the time goes in v3:
time: 82.4 us; the launch traced here: 81.9 us
  blocking collectives  39.2 us (48%)
  waiting for transfers between devices  24.3 us (29%)
  starting transfers between devices  10.5 us (13%)
  Pallas kernels  6.52 us (8%)
  between operations  1.38 us (2%)
    ppermute x1, waiting for transfers between devices, per_device(): lax.ppermute(own, GRID, [(i, (i + 1) % blocks) for i in range(blocks)])  18.8 us
    all_to_all x1, blocking collectives, per_device(): field = lax.all_to_all(evolved, 'y', 0, 0, tiled=True)  14.6 us
    all_to_all x1, blocking collectives, per_device(): parts = lax.all_to_all(part, ('core', 'y'), 0, 0, tiled=True)  13.5 us
    all_to_all x1, blocking collectives, per_device(): parts = lax.all_to_all(part, 'x', 0, 0, tiled=True)  11.1 us
    all_to_all x1, starting transfers between devices, per_device(): parts = lax.all_to_all(part, 'z', 0, 0, tiled=True)  6.65 us
    pallas_call x7, Pallas kernels, call(): pl.pallas_call(body, out_shape=outs, in_specs=[pl.BlockSpec(memory_space=...  6.52 us
    all_to_all x1, waiting for transfers between devices, per_device(): parts = lax.all_to_all(part, 'z', 0, 0, tiled=True)  3.97 us
    ppermute x1, starting transfers between devices, per_device(): lax.ppermute(own, GRID, [(i, (i + 1) % blocks) for i in range(blocks)])  1.92 us
  transfers between devices with their start and end apart: 3, of which 3 were waited for; matrix products, arithmetic and copies ran while one was open for 0% of the time, Pallas kernels for 2%

profile of v3, /device:TPU:16, one launch (start us, length us, event | category | flops | bytes accessed | tf_op | source)
XLA Modules:
  0.0 81.9 jit_solution(4747806701644991269)
XLA Ops:
  0.6 1.0 %pack_block.1.own = f32[13,8,256]{2,1,0:T(8,128)S(1)} custom-call(f32[8,8,256]{2,1,0:T(8,128)} %bitcast.18, f32[16,256]{1,0:T(8,128)} %bitcast.20, s32[8,256]{1,0:T(8,128)} %col.1, f32[8,256]{1,0:T(8,128)} %bitcast.21, s32[8,8,8]{2,1,0:T(8,128)} %mask.1), custom_call_target="tpu_custom_call" | custom-call | flops 1000000 | bytes 206848 | tf_op jit(solution)/shard_map/pack_block/pallas_call | solution.py:24
  1.6 1.9 %collective-permute-start = (f32[13,8,256]{2,1,0:T(8,128)S(1)}, f32[13,8,256]{2,1,0:T(8,128)S(1)}, u32[]{:S(2)}, u32[]{:S(2)}) collective-permute-start(f32[13,8,256]{2,1,0:T(8,128)S(1)} %pack_block.1.own), channel_id=1, source_target_pairs={{0,8},{8,16},{16,24},{24,32},{32,40},{40,48},{48,56},{56,64},{64,7... | collective-permute-start | bytes 319496 | tf_op jit(solution)/shard_map/ppermute | solution.py:312
  3.6 0.0 copy-start
  4.2 0.0 copy-done
  4.3 18.8 %collective-permute-done.low = f32[13,8,256]{2,1,0:T(8,128)S(1)} collective-permute-done((f32[13,8,256]{2,1,0:T(8,128)S(1)}, f32[13,8,256]{2,1,0:T(8,128)S(1)}, u32[]{:S(2)}, u32[]{:S(2)}) %collective-permute-start) | collective-permute-done | bytes 106528 | tf_op jit(solution)/shard_map/ppermute | solution.py:312
  23.1 0.5 tangent.1
  23.5 14.6 %all_to_all.20.field = f32[8,8,256]{2,1,0:T(8,128)S(1)} all-to-all(f32[8,8,256]{2,1,0:T(8,128)S(1)} %get-tuple-element.10), channel_id=1, replica_groups=mesh['z'=8,'x'=8,'core'=2,'y'=8] {'y'}, dimensions={0} | all-to-all | bytes 131072 | tf_op jit(solution)/shard_map/all_to_all | solution.py:332
  38.1 0.3 gram_block.1
  38.5 13.5 %all_to_all.21 = f32[16,24,128]{2,1,0:T(8,128)S(1)} all-to-all(f32[16,24,128]{2,1,0:T(8,128)S(1)} %gram_block.1), channel_id=1, replica_groups=mesh['z'=8,'x'=8,'core'=2,'y'=8] {'core','y'}, dimensions={0} | all-to-all | bytes 393216 | tf_op jit(solution)/shard_map/all_to_all | solution.py:334
  52.0 0.1 first_sum.1
  52.1 11.1 %all_to_all.22.parts = f32[8,24,128]{2,1,0:T(8,128)S(1)} all-to-all(f32[8,24,128]{2,1,0:T(8,128)S(1)} %get-tuple-element.13), channel_id=1, replica_groups=mesh['z'=8,'x'=8,'core'=2,'y'=8] {'x'}, dimensions={0} | all-to-all | bytes 196608 | tf_op jit(solution)/shard_map/all_to_all | solution.py:342
  63.2 0.6 next_sum.1
  63.8 6.6 %all-to-all-start.3 = ((f32[8,24,128]{2,1,0:T(8,128)}), f32[8,24,128]{2,1,0:T(8,128)S(1)}, u32[]{:S(2)}, u32[]{:S(2)}) async-start(f32[8,24,128]{2,1,0:T(8,128)} %next_sum.1), calls=%async_computation.3 | async-start | bytes 196608 | tf_op jit(solution)/shard_map/all_to_all | solution.py:344
  70.5 1.9 %collective-permute-start.1 = (f32[4,8,256]{2,1,0:T(8,128)S(1)}, f32[4,8,256]{2,1,0:T(8,128)S(1)}, u32[]{:S(2)}, u32[]{:S(2)}) collective-permute-start(f32[4,8,256]{2,1,0:T(8,128)S(1)} %get-tuple-element.16.window), channel_id=1, source_target_pairs={{8,0},{16,8},{24,16},{32,24},{40,32},{48,40},{56,48},{64,56},{72,6... | collective-permute-start | bytes 98312 | tf_op jit(solution)/shard_map/ppermute | solution.py:345
  72.4 1.6 %collective-permute-done.1.beyond = f32[4,8,256]{2,1,0:T(8,128)S(1)} collective-permute-done((f32[4,8,256]{2,1,0:T(8,128)S(1)}, f32[4,8,256]{2,1,0:T(8,128)S(1)}, u32[]{:S(2)}, u32[]{:S(2)}) %collective-permute-start.1) | collective-permute-done | bytes 32800 | tf_op jit(solution)/shard_map/ppermute | solution.py:345
  73.9 1.3 %adjoint.1 = f32[8,8,256]{2,1,0:T(8,128)} custom-call(f32[13,8,256]{2,1,0:T(8,128)S(1)} %collective-permute-done.low, f32[13,8,256]{2,1,0:T(8,128)S(1)} %pack_block.1.own, f32[4,8,256]{2,1,0:T(8,128)S(1)} %get-tuple-element.16.window, f32[4,8,256]{2,1,0:T(8,128)S(1)} %collective-permute-done.1.beyond, f32[1,1]{1,0:T(1,128)} %bitcast.16.kappa, ...), custom_call_target="tpu_custom_call" | custom-call | flops 1000000 | bytes 344076 | tf_op jit(solution)/shard_map/adjoint/pallas_call | solution.py:24
  75.2 4.0 %all-to-all-done.3.parts = f32[8,24,128]{2,1,0:T(8,128)S(1)} async-done(((f32[8,24,128]{2,1,0:T(8,128)}), f32[8,24,128]{2,1,0:T(8,128)S(1)}, u32[]{:S(2)}, u32[]{:S(2)}) %all-to-all-start.3) | async-done | bytes 98336 | tf_op jit(solution)/shard_map/all_to_all | solution.py:344
  79.2 2.8 %newton_step.1 = (f32[64,64]{1,0:T(8,128)}, f32[1,64]{1,0:T(1,128)}) custom-call(f32[8,24,128]{2,1,0:T(8,128)S(1)} %all-to-all-done.3.parts, f32[1,128]{1,0:T(1,128)S(1)} %pad_bitcast_fusion.alpha), custom_call_target="tpu_custom_call" | custom-call | flops 1000000 | bytes 115456 | tf_op jit(solution)/shard_map/newton_step/pallas_call | solution.py:24
  (1 shorter events, 0.0 us)
Async XLA Ops:
  1.6 21.4 %collective-permute-start = (f32[13,8,256]{2,1,0:T(8,128)S(1)}, f32[13,8,256]{2,1,0:T(8,128)S(1)}, u32[]{:S(2)}, u32[]{:S(2)}) collective-permute-start(f32[13,8,256]{2,1,0:T(8,128)S(1)} %pack_block.1.own), channel_id=1, source_target_pairs={{0,8},{8,16},{16,24},{24,32},{32,40},{40,48},{48,56},{56,64},{64,7... | collective-permute-start | bytes 319496 | tf_op jit(solution)/shard_map/ppermute | solution.py:312
  3.6 0.7 copy-start
  63.8 15.4 %all-to-all-start.3 = ((f32[8,24,128]{2,1,0:T(8,128)}), f32[8,24,128]{2,1,0:T(8,128)S(1)}, u32[]{:S(2)}, u32[]{:S(2)}) async-start(f32[8,24,128]{2,1,0:T(8,128)} %next_sum.1), calls=%async_computation.3 | async-start | bytes 196608 | tf_op jit(solution)/shard_map/all_to_all | solution.py:344
  70.5 3.5 %collective-permute-start.1 = (f32[4,8,256]{2,1,0:T(8,128)S(1)}, f32[4,8,256]{2,1,0:T(8,128)S(1)}, u32[]{:S(2)}, u32[]{:S(2)}) collective-permute-start(f32[4,8,256]{2,1,0:T(8,128)S(1)} %get-tuple-element.16.window), channel_id=1, source_target_pairs={{8,0},{16,8},{24,16},{32,24},{40,32},{48,40},{56,48},{64,56},{72,6... | collective-permute-start | bytes 98312 | tf_op jit(solution)/shard_map/ppermute | solution.py:345

commit v4 on v3

--- a/solution.py
+++ b/solution.py
@@ -12,7 +12,8 @@
 F32 = jnp.float32
 HI = lax.Precision.HIGHEST
 GRID = ("z", "x", "core")
-PACK = 24
+CORE = 17 * 128
+PACK = CORE + 256
 
 
 def vmem():
@@ -182,14 +183,10 @@
     packed = jnp.where((j < 32) & (i > j), low, top)
     on_diagonal = iota2((32, 128), 1) == iota2((32, 128), 0) + 96
     diagonal = jnp.sum(jnp.where(on_diagonal, g[32:64], 0.0), axis=0, keepdims=True)
-    sub = iota2((8, 128), 0)
-    extra = jnp.where(iota2((8, 128), 1) < 64, g[64:72], diagonal)
-    tail = extra
-    for h in range(2):
-        tail = jnp.where(sub == h + 1, forcing[:, 128 * h : 128 * h + 128], tail)
+    extra = jnp.where(iota2((1, 128), 1) < 64, g[64:65], diagonal)
+    flat = jnp.concatenate([packed[r : r + 1] for r in range(16)] + [extra, forcing], axis=1)
     for c in range(copies):
-        out[c, 0:16, :] = packed
-        out[c, 16:24, :] = tail
+        out[c] = flat
 
 
 def sum_blocks(parts):
@@ -200,17 +197,15 @@
 
 
 def first_sum(parts, own, core, out, window):
-    rows = parts.shape[0] // 2
-    total = parts[0:PACK, :]
-    for c in range(1, parts.shape[0] // PACK):
-        total = total + parts[PACK * c : PACK * c + PACK, :]
+    half = parts.shape[0] // 2
+    total = sum_blocks(parts)[:, 0:CORE]
     for c in range(out.shape[0]):
         out[c] = total
     odd = core[...] > 0.5
-    for h in range(2):
-        a = parts[pl.ds(17 + h, 8, stride=PACK), :]
-        b = parts[pl.ds(17 + h + rows, 8, stride=PACK), :]
-        window[0, :, 128 * h : 128 * h + 128] = jnp.where(odd, b, a)
+    for y in range(8):
+        window[0, y : y + 1, :] = jnp.where(
+            odd, parts[half + y][:, CORE:PACK], parts[y][:, CORE:PACK]
+        )
     window[1] = own[8]
     window[2] = own[9]
     window[3] = own[12]
@@ -232,7 +227,8 @@
 
 def newton_step(count, parts, alpha, factor, newton):
     total = sum_blocks(parts)
-    packed, extra = total[0:16], total[16:17]
+    packed = jnp.concatenate([total[:, 128 * r : 128 * r + 128] for r in range(16)], axis=0)
+    extra = total[:, CORE - 128 : CORE]
     lane, sub = iota2((32, 128), 1), iota2((32, 128), 0)
     s = jnp.concatenate([packed, pltpu.roll(packed, 64, 1)], axis=0)
     top = jnp.where((lane >= sub) & (lane < 64), s, 0.0)
@@ -330,17 +326,17 @@
         follows,
     )
     field = lax.all_to_all(evolved, "y", 0, 0, tiled=True)
-    (part,) = call(gram_block, [shape(2 * ny, PACK, 128)], field, binned, column)
+    (part,) = call(gram_block, [shape(2 * ny, 1, PACK)], field, binned, column)
     parts = lax.all_to_all(part, ("core", "y"), 0, 0, tiled=True)
     part, window = call(
         first_sum,
-        [shape(lax.axis_size("x"), PACK, 128), shape(4, 8, 256)],
-        parts.reshape(-1, 128),
+        [shape(lax.axis_size("x"), 1, CORE), shape(4, 8, 256)],
+        parts,
         own,
         core,
     )
     parts = lax.all_to_all(part, "x", 0, 0, tiled=True)
-    (part,) = call(next_sum, [shape(lax.axis_size("z"), PACK, 128)], parts)
+    (part,) = call(next_sum, [shape(lax.axis_size("z"), 1, CORE)], parts)
     parts = lax.all_to_all(part, "z", 0, 0, tiled=True)
     beyond = lax.ppermute(window, GRID, [((i + 1) % blocks, i) for i in range(blocks)])
     (sens,) = call(

time: 82.4 us -> 80.8 us (0.981)
  blocking collectives: 39.2 us -> 38 us
    all_to_all x1, blocking collectives: 13.5 us -> 12.6 us  [per_device(): parts = lax.all_to_all(part, ('core', 'y'), 0, 0, tiled=True)]
where the time goes in v4:
time: 80.8 us; the launch traced here: 80.4 us
  blocking collectives  38 us (47%)
  waiting for transfers between devices  24 us (30%)
  starting transfers between devices  10.5 us (13%)
  Pallas kernels  6.52 us (8%)
  between operations  1.38 us (2%)
    ppermute x1, waiting for transfers between devices, per_device(): lax.ppermute(own, GRID, [(i, (i + 1) % blocks) for i in range(blocks)])  18.8 us
    all_to_all x1, blocking collectives, per_device(): field = lax.all_to_all(evolved, 'y', 0, 0, tiled=True)  14.6 us
    all_to_all x1, blocking collectives, per_device(): parts = lax.all_to_all(part, ('core', 'y'), 0, 0, tiled=True)  12.6 us
    all_to_all x1, blocking collectives, per_device(): parts = lax.all_to_all(part, 'x', 0, 0, tiled=True)  10.8 us
    all_to_all x1, starting transfers between devices, per_device(): parts = lax.all_to_all(part, 'z', 0, 0, tiled=True)  6.65 us
    pallas_call x7, Pallas kernels, call(): pl.pallas_call(body, out_shape=outs, in_specs=[pl.BlockSpec(memory_space=...  6.52 us
    all_to_all x1, waiting for transfers between devices, per_device(): parts = lax.all_to_all(part, 'z', 0, 0, tiled=True)  3.66 us
    ppermute x1, starting transfers between devices, per_device(): lax.ppermute(own, GRID, [(i, (i + 1) % blocks) for i in range(blocks)])  1.92 us
  transfers between devices with their start and end apart: 3, of which 3 were waited for; matrix products, arithmetic and copies ran while one was open for 0% of the time, Pallas kernels for 2%

profile of v4, /device:TPU:16, one launch (start us, length us, event | category | flops | bytes accessed | tf_op | source)
XLA Modules:
  0.0 80.4 jit_solution(5632943112423310445)
XLA Ops:
  0.6 1.0 %pack_block.1.own = f32[13,8,256]{2,1,0:T(8,128)S(1)} custom-call(f32[8,8,256]{2,1,0:T(8,128)} %bitcast.16, f32[16,256]{1,0:T(8,128)} %bitcast.18, s32[8,256]{1,0:T(8,128)} %col.1, f32[8,256]{1,0:T(8,128)} %bitcast.19, s32[8,8,8]{2,1,0:T(8,128)} %mask.1), custom_call_target="tpu_custom_call" | custom-call | flops 1000000 | bytes 206848 | tf_op jit(solution)/shard_map/pack_block/pallas_call | solution.py:25
  1.6 1.9 %collective-permute-start = (f32[13,8,256]{2,1,0:T(8,128)S(1)}, f32[13,8,256]{2,1,0:T(8,128)S(1)}, u32[]{:S(2)}, u32[]{:S(2)}) collective-permute-start(f32[13,8,256]{2,1,0:T(8,128)S(1)} %pack_block.1.own), channel_id=1, source_target_pairs={{0,8},{8,16},{16,24},{24,32},{32,40},{40,48},{48,56},{56,64},{64,7... | collective-permute-start | bytes 319496 | tf_op jit(solution)/shard_map/ppermute | solution.py:308
  3.6 0.0 copy-start
  4.2 0.0 copy-done
  4.3 18.8 %collective-permute-done.low = f32[13,8,256]{2,1,0:T(8,128)S(1)} collective-permute-done((f32[13,8,256]{2,1,0:T(8,128)S(1)}, f32[13,8,256]{2,1,0:T(8,128)S(1)}, u32[]{:S(2)}, u32[]{:S(2)}) %collective-permute-start) | collective-permute-done | bytes 106528 | tf_op jit(solution)/shard_map/ppermute | solution.py:308
  23.1 0.5 tangent.1
  23.5 14.6 %all_to_all.20.field = f32[8,8,256]{2,1,0:T(8,128)S(1)} all-to-all(f32[8,8,256]{2,1,0:T(8,128)S(1)} %get-tuple-element.10), channel_id=1, replica_groups=mesh['z'=8,'x'=8,'core'=2,'y'=8] {'y'}, dimensions={0} | all-to-all | bytes 131072 | tf_op jit(solution)/shard_map/all_to_all | solution.py:328
  38.1 0.3 gram_block.1
  38.5 12.6 %all_to_all.21.parts = f32[16,1,2432]{2,1,0:T(1,128)S(1)} all-to-all(f32[16,1,2432]{2,1,0:T(1,128)S(1)} %gram_block.1), channel_id=1, replica_groups=mesh['z'=8,'x'=8,'core'=2,'y'=8] {'core','y'}, dimensions={0} | all-to-all | bytes 311296 | tf_op jit(solution)/shard_map/all_to_all | solution.py:330
  51.1 0.1 first_sum.1
  51.2 10.8 %all_to_all.22.parts = f32[8,1,2176]{2,1,0:T(1,128)S(1)} all-to-all(f32[8,1,2176]{2,1,0:T(1,128)S(1)} %get-tuple-element.13), channel_id=1, replica_groups=mesh['z'=8,'x'=8,'core'=2,'y'=8] {'x'}, dimensions={0} | all-to-all | bytes 139264 | tf_op jit(solution)/shard_map/all_to_all | solution.py:338
  61.9 0.6 next_sum.1
  62.6 6.7 %all-to-all-start.3 = ((f32[8,1,2176]{2,1,0:T(1,128)}), f32[8,1,2176]{2,1,0:T(1,128)S(1)}, u32[]{:S(2)}, u32[]{:S(2)}) async-start(f32[8,1,2176]{2,1,0:T(1,128)} %next_sum.1), calls=%async_computation.3 | async-start | bytes 139264 | tf_op jit(solution)/shard_map/all_to_all | solution.py:340
  69.2 1.9 %collective-permute-start.1 = (f32[4,8,256]{2,1,0:T(8,128)S(1)}, f32[4,8,256]{2,1,0:T(8,128)S(1)}, u32[]{:S(2)}, u32[]{:S(2)}) collective-permute-start(f32[4,8,256]{2,1,0:T(8,128)S(1)} %get-tuple-element.16.window), channel_id=1, source_target_pairs={{8,0},{16,8},{24,16},{32,24},{40,32},{48,40},{56,48},{64,56},{72,6... | collective-permute-start | bytes 98312 | tf_op jit(solution)/shard_map/ppermute | solution.py:341
  71.1 1.6 %collective-permute-done.1.beyond = f32[4,8,256]{2,1,0:T(8,128)S(1)} collective-permute-done((f32[4,8,256]{2,1,0:T(8,128)S(1)}, f32[4,8,256]{2,1,0:T(8,128)S(1)}, u32[]{:S(2)}, u32[]{:S(2)}) %collective-permute-start.1) | collective-permute-done | bytes 32800 | tf_op jit(solution)/shard_map/ppermute | solution.py:341
  72.7 1.3 %adjoint.1 = f32[8,8,256]{2,1,0:T(8,128)} custom-call(f32[13,8,256]{2,1,0:T(8,128)S(1)} %collective-permute-done.low, f32[13,8,256]{2,1,0:T(8,128)S(1)} %pack_block.1.own, f32[4,8,256]{2,1,0:T(8,128)S(1)} %get-tuple-element.16.window, f32[4,8,256]{2,1,0:T(8,128)S(1)} %collective-permute-done.1.beyond, f32[1,1]{1,0:T(1,128)} %bitcast.15.kappa, ...), custom_call_target="tpu_custom_call" | custom-call | flops 1000000 | bytes 344076 | tf_op jit(solution)/shard_map/adjoint/pallas_call | solution.py:25
  74.0 3.7 %all-to-all-done.3.parts = f32[8,1,2176]{2,1,0:T(1,128)S(1)} async-done(((f32[8,1,2176]{2,1,0:T(1,128)}), f32[8,1,2176]{2,1,0:T(1,128)S(1)}, u32[]{:S(2)}, u32[]{:S(2)}) %all-to-all-start.3) | async-done | bytes 69664 | tf_op jit(solution)/shard_map/all_to_all | solution.py:340
  77.7 2.8 %newton_step.1 = (f32[64,64]{1,0:T(8,128)}, f32[1,64]{1,0:T(1,128)}) custom-call(f32[8,1,2176]{2,1,0:T(1,128)S(1)} %all-to-all-done.3.parts, f32[1,128]{1,0:T(1,128)S(1)} %pad_bitcast_fusion.alpha), custom_call_target="tpu_custom_call" | custom-call | flops 1000000 | bytes 86784 | tf_op jit(solution)/shard_map/newton_step/pallas_call | solution.py:25
  (1 shorter events, 0.0 us)
Async XLA Ops:
  1.6 21.4 %collective-permute-start = (f32[13,8,256]{2,1,0:T(8,128)S(1)}, f32[13,8,256]{2,1,0:T(8,128)S(1)}, u32[]{:S(2)}, u32[]{:S(2)}) collective-permute-start(f32[13,8,256]{2,1,0:T(8,128)S(1)} %pack_block.1.own), channel_id=1, source_target_pairs={{0,8},{8,16},{16,24},{24,32},{32,40},{40,48},{48,56},{56,64},{64,7... | collective-permute-start | bytes 319496 | tf_op jit(solution)/shard_map/ppermute | solution.py:308
  3.6 0.7 copy-start
  62.6 15.1 %all-to-all-start.3 = ((f32[8,1,2176]{2,1,0:T(1,128)}), f32[8,1,2176]{2,1,0:T(1,128)S(1)}, u32[]{:S(2)}, u32[]{:S(2)}) async-start(f32[8,1,2176]{2,1,0:T(1,128)} %next_sum.1), calls=%async_computation.3 | async-start | bytes 139264 | tf_op jit(solution)/shard_map/all_to_all | solution.py:340
  69.2 3.5 %collective-permute-start.1 = (f32[4,8,256]{2,1,0:T(8,128)S(1)}, f32[4,8,256]{2,1,0:T(8,128)S(1)}, u32[]{:S(2)}, u32[]{:S(2)}) collective-permute-start(f32[4,8,256]{2,1,0:T(8,128)S(1)} %get-tuple-element.16.window), channel_id=1, source_target_pairs={{8,0},{16,8},{24,16},{32,24},{40,32},{48,40},{56,48},{64,56},{72,6... | collective-permute-start | bytes 98312 | tf_op jit(solution)/shard_map/ppermute | solution.py:341

commit v5 on v4

--- a/solution.py
+++ b/solution.py
@@ -13,7 +13,8 @@
 HI = lax.Precision.HIGHEST
 GRID = ("z", "x", "core")
 CORE = 17 * 128
-PACK = CORE + 256
+HALF = 9 * 128
+PACK = HALF + 256
 
 
 def vmem():
@@ -184,27 +185,28 @@
     on_diagonal = iota2((32, 128), 1) == iota2((32, 128), 0) + 96
     diagonal = jnp.sum(jnp.where(on_diagonal, g[32:64], 0.0), axis=0, keepdims=True)
     extra = jnp.where(iota2((1, 128), 1) < 64, g[64:65], diagonal)
-    flat = jnp.concatenate([packed[r : r + 1] for r in range(16)] + [extra, forcing], axis=1)
+    lines = [packed[r : r + 1] for r in range(16)] + [extra]
+    halves = [jnp.concatenate(lines[h : h + 9] + [forcing], axis=1) for h in (0, 8)]
     for c in range(copies):
-        out[c] = flat
-
-
-def sum_blocks(parts):
-    total = parts[0]
-    for c in range(1, parts.shape[0]):
+        out[c] = halves[2 * c // copies]
+
+
+def sum_blocks(parts, first=0, stride=1):
+    total = parts[first]
+    for c in range(first + stride, parts.shape[0], stride):
         total = total + parts[c]
     return total
 
 
 def first_sum(parts, own, core, out, window):
     half = parts.shape[0] // 2
-    total = sum_blocks(parts)[:, 0:CORE]
+    total = sum_blocks(parts)[:, 0:HALF]
     for c in range(out.shape[0]):
         out[c] = total
     odd = core[...] > 0.5
     for y in range(8):
         window[0, y : y + 1, :] = jnp.where(
-            odd, parts[half + y][:, CORE:PACK], parts[y][:, CORE:PACK]
+            odd, parts[half + y][:, HALF:PACK], parts[y][:, HALF:PACK]
         )
     window[1] = own[8]
     window[2] = own[9]
@@ -226,7 +228,8 @@
 
 
 def newton_step(count, parts, alpha, factor, newton):
-    total = sum_blocks(parts)
+    upper, lower = sum_blocks(parts, 0, 2), sum_blocks(parts, 1, 2)
+    total = jnp.concatenate([upper, lower[:, 128:HALF]], axis=1)
     packed = jnp.concatenate([total[:, 128 * r : 128 * r + 128] for r in range(16)], axis=0)
     extra = total[:, CORE - 128 : CORE]
     lane, sub = iota2((32, 128), 1), iota2((32, 128), 0)
@@ -330,14 +333,14 @@
     parts = lax.all_to_all(part, ("core", "y"), 0, 0, tiled=True)
     part, window = call(
         first_sum,
-        [shape(lax.axis_size("x"), 1, CORE), shape(4, 8, 256)],
+        [shape(lax.axis_size("x"), 1, HALF), shape(4, 8, 256)],
         parts,
         own,
         core,
     )
     parts = lax.all_to_all(part, "x", 0, 0, tiled=True)
-    (part,) = call(next_sum, [shape(lax.axis_size("z"), 1, CORE)], parts)
-    parts = lax.all_to_all(part, "z", 0, 0, tiled=True)
+    (part,) = call(next_sum, [shape(2 * lax.axis_size("z"), 1, HALF)], parts)
+    parts = lax.all_to_all(part, ("z", "core"), 0, 0, tiled=True)
     beyond = lax.ppermute(window, GRID, [((i + 1) % blocks, i) for i in range(blocks)])
     (sens,) = call(
         adjoint, [shape(8, 8, 256)], low, own, window, beyond, k, joined, follows

time: 80.8 us -> 80.8 us (level)
  the two profiles are of different devices: /device:TPU:16 before, /device:TPU:1 now
where the time goes in v5:
time: 80.8 us; the launch traced here: 80.4 us
  blocking collectives  40.8 us (50%)
  waiting for transfers between devices  16.3 us (20%)
  starting transfers between devices  15.4 us (19%)
  Pallas kernels  6.53 us (8%)
  between operations  1.38 us (2%)
    all_to_all x1, blocking collectives, per_device(): parts = lax.all_to_all(part, ('core', 'y'), 0, 0, tiled=True)  21.9 us
    ppermute x1, waiting for transfers between devices, per_device(): lax.ppermute(own, GRID, [(i, (i + 1) % blocks) for i in range(blocks)])  11.6 us
    all_to_all x1, blocking collectives, per_device(): field = lax.all_to_all(evolved, 'y', 0, 0, tiled=True)  9.6 us
    all_to_all x1, blocking collectives, per_device(): parts = lax.all_to_all(part, 'x', 0, 0, tiled=True)  9.28 us
    all_to_all x1, starting transfers between devices, per_device(): parts = lax.all_to_all(part, ('z', 'core'), 0, 0, tiled=True)  8.91 us
    pallas_call x7, Pallas kernels, call(): pl.pallas_call(body, out_shape=outs, in_specs=[pl.BlockSpec(memory_space=...  6.53 us
    ppermute x1, starting transfers between devices, per_device(): lax.ppermute(own, GRID, [(i, (i + 1) % blocks) for i in range(blocks)])  4.5 us
    ppermute x1, waiting for transfers between devices, per_device(): lax.ppermute(window, GRID, [((i + 1) % blocks, i) for i in range(blocks)])  3.5 us
  transfers between devices with their start and end apart: 3, of which 3 were waited for; matrix products, arithmetic and copies ran while one was open for 0% of the time, Pallas kernels for 2%

profile of v5, /device:TPU:1, one launch (start us, length us, event | category | flops | bytes accessed | tf_op | source)
XLA Modules:
  0.0 80.4 jit_solution(12517812113815439219)
XLA Ops:
  0.6 1.0 %pack_block.1.own = f32[13,8,256]{2,1,0:T(8,128)S(1)} custom-call(f32[8,8,256]{2,1,0:T(8,128)} %bitcast.16, f32[16,256]{1,0:T(8,128)} %bitcast.18, s32[8,256]{1,0:T(8,128)} %col.1, f32[8,256]{1,0:T(8,128)} %bitcast.19, s32[8,8,8]{2,1,0:T(8,128)} %mask.1), custom_call_target="tpu_custom_call" | custom-call | flops 1000000 | bytes 206848 | tf_op jit(solution)/shard_map/pack_block/pallas_call | solution.py:26
  1.6 4.5 %collective-permute-start = (f32[13,8,256]{2,1,0:T(8,128)S(1)}, f32[13,8,256]{2,1,0:T(8,128)S(1)}, u32[]{:S(2)}, u32[]{:S(2)}) collective-permute-start(f32[13,8,256]{2,1,0:T(8,128)S(1)} %pack_block.1.own), channel_id=1, source_target_pairs={{0,8},{8,16},{16,24},{24,32},{32,40},{40,48},{48,56},{56,64},{64,7... | collective-permute-start | bytes 319496 | tf_op jit(solution)/shard_map/ppermute | solution.py:311
  6.1 0.0 copy-start
  6.8 0.0 copy-done
  6.8 11.6 %collective-permute-done.low = f32[13,8,256]{2,1,0:T(8,128)S(1)} collective-permute-done((f32[13,8,256]{2,1,0:T(8,128)S(1)}, f32[13,8,256]{2,1,0:T(8,128)S(1)}, u32[]{:S(2)}, u32[]{:S(2)}) %collective-permute-start) | collective-permute-done | bytes 106528 | tf_op jit(solution)/shard_map/ppermute | solution.py:311
  18.4 0.5 tangent.1
  18.9 9.6 %all_to_all.20.field = f32[8,8,256]{2,1,0:T(8,128)S(1)} all-to-all(f32[8,8,256]{2,1,0:T(8,128)S(1)} %get-tuple-element.10), channel_id=1, replica_groups=mesh['z'=8,'x'=8,'core'=2,'y'=8] {'y'}, dimensions={0} | all-to-all | bytes 131072 | tf_op jit(solution)/shard_map/all_to_all | solution.py:331
  28.5 0.3 gram_block.1
  28.9 21.9 %all_to_all.21.parts = f32[16,1,1408]{2,1,0:T(1,128)S(1)} all-to-all(f32[16,1,1408]{2,1,0:T(1,128)S(1)} %gram_block.1), channel_id=1, replica_groups=mesh['z'=8,'x'=8,'core'=2,'y'=8] {'core','y'}, dimensions={0} | all-to-all | bytes 180224 | tf_op jit(solution)/shard_map/all_to_all | solution.py:333
  50.8 0.1 first_sum.1
  50.9 9.3 %all_to_all.22.parts = f32[8,1,1152]{2,1,0:T(1,128)S(1)} all-to-all(f32[8,1,1152]{2,1,0:T(1,128)S(1)} %get-tuple-element.13), channel_id=1, replica_groups=mesh['z'=8,'x'=8,'core'=2,'y'=8] {'x'}, dimensions={0} | all-to-all | bytes 73728 | tf_op jit(solution)/shard_map/all_to_all | solution.py:341
  60.1 0.6 next_sum.1
  60.8 8.9 %all-to-all-start.3 = ((f32[16,1,1152]{2,1,0:T(1,128)}), f32[16,1,1152]{2,1,0:T(1,128)S(1)}, u32[]{:S(2)}, u32[]{:S(2)}) async-start(f32[16,1,1152]{2,1,0:T(1,128)} %next_sum.1), calls=%async_computation.3 | async-start | bytes 147456 | tf_op jit(solution)/shard_map/all_to_all | solution.py:343
  69.7 2.0 %collective-permute-start.1 = (f32[4,8,256]{2,1,0:T(8,128)S(1)}, f32[4,8,256]{2,1,0:T(8,128)S(1)}, u32[]{:S(2)}, u32[]{:S(2)}) collective-permute-start(f32[4,8,256]{2,1,0:T(8,128)S(1)} %get-tuple-element.16.window), channel_id=1, source_target_pairs={{8,0},{16,8},{24,16},{32,24},{40,32},{48,40},{56,48},{64,56},{72,6... | collective-permute-start | bytes 98312 | tf_op jit(solution)/shard_map/ppermute | solution.py:344
  71.7 3.5 %collective-permute-done.1.beyond = f32[4,8,256]{2,1,0:T(8,128)S(1)} collective-permute-done((f32[4,8,256]{2,1,0:T(8,128)S(1)}, f32[4,8,256]{2,1,0:T(8,128)S(1)}, u32[]{:S(2)}, u32[]{:S(2)}) %collective-permute-start.1) | collective-permute-done | bytes 32800 | tf_op jit(solution)/shard_map/ppermute | solution.py:344
  75.2 1.3 %adjoint.1 = f32[8,8,256]{2,1,0:T(8,128)} custom-call(f32[13,8,256]{2,1,0:T(8,128)S(1)} %collective-permute-done.low, f32[13,8,256]{2,1,0:T(8,128)S(1)} %pack_block.1.own, f32[4,8,256]{2,1,0:T(8,128)S(1)} %get-tuple-element.16.window, f32[4,8,256]{2,1,0:T(8,128)S(1)} %collective-permute-done.1.beyond, f32[1,1]{1,0:T(1,128)} %bitcast.15.kappa, ...), custom_call_target="tpu_custom_call" | custom-call | flops 1000000 | bytes 344076 | tf_op jit(solution)/shard_map/adjoint/pallas_call | solution.py:26
  76.5 1.2 %all-to-all-done.3.parts = f32[16,1,1152]{2,1,0:T(1,128)S(1)} async-done(((f32[16,1,1152]{2,1,0:T(1,128)}), f32[16,1,1152]{2,1,0:T(1,128)S(1)}, u32[]{:S(2)}, u32[]{:S(2)}) %all-to-all-start.3) | async-done | bytes 73760 | tf_op jit(solution)/shard_map/all_to_all | solution.py:343
  77.6 2.8 %newton_step.1 = (f32[64,64]{1,0:T(8,128)}, f32[1,64]{1,0:T(1,128)}) custom-call(f32[16,1,1152]{2,1,0:T(1,128)S(1)} %all-to-all-done.3.parts, f32[1,128]{1,0:T(1,128)S(1)} %pad_bitcast_fusion.alpha), custom_call_target="tpu_custom_call" | custom-call | flops 1000000 | bytes 90880 | tf_op jit(solution)/shard_map/newton_step/pallas_call | solution.py:26
  (1 shorter events, 0.0 us)
Async XLA Ops:
  1.6 16.8 %collective-permute-start = (f32[13,8,256]{2,1,0:T(8,128)S(1)}, f32[13,8,256]{2,1,0:T(8,128)S(1)}, u32[]{:S(2)}, u32[]{:S(2)}) collective-permute-start(f32[13,8,256]{2,1,0:T(8,128)S(1)} %pack_block.1.own), channel_id=1, source_target_pairs={{0,8},{8,16},{16,24},{24,32},{32,40},{40,48},{48,56},{56,64},{64,7... | collective-permute-start | bytes 319496 | tf_op jit(solution)/shard_map/ppermute | solution.py:311
  6.1 0.7 copy-start
  60.8 16.8 %all-to-all-start.3 = ((f32[16,1,1152]{2,1,0:T(1,128)}), f32[16,1,1152]{2,1,0:T(1,128)S(1)}, u32[]{:S(2)}, u32[]{:S(2)}) async-start(f32[16,1,1152]{2,1,0:T(1,128)} %next_sum.1), calls=%async_computation.3 | async-start | bytes 147456 | tf_op jit(solution)/shard_map/all_to_all | solution.py:343
  69.7 5.5 %collective-permute-start.1 = (f32[4,8,256]{2,1,0:T(8,128)S(1)}, f32[4,8,256]{2,1,0:T(8,128)S(1)}, u32[]{:S(2)}, u32[]{:S(2)}) collective-permute-start(f32[4,8,256]{2,1,0:T(8,128)S(1)} %get-tuple-element.16.window), channel_id=1, source_target_pairs={{8,0},{16,8},{24,16},{32,24},{40,32},{48,40},{56,48},{64,56},{72,6... | collective-permute-start | bytes 98312 | tf_op jit(solution)/shard_map/ppermute | solution.py:344

commit v6 on v5

--- a/solution.py
+++ b/solution.py
@@ -289,6 +289,13 @@
     newton[...] = pltpu.roll(solved, 64, 1)[0:1, 0:64]
 
 
+def finish(
+    count, parts, alpha, low, own, window, beyond, kappa, joined, follows, factor, newton, sens
+):
+    adjoint(low, own, window, beyond, kappa, joined, follows, sens)
+    newton_step(count, parts, alpha, factor, newton)
+
+
 def per_device(perturb, winds, kappa, obs_col, innov, alpha, loc_mask):
     ny = lax.axis_size("y")
     blocks = lax.axis_size(GRID)
@@ -342,12 +349,21 @@
     (part,) = call(next_sum, [shape(2 * lax.axis_size("z"), 1, HALF)], parts)
     parts = lax.all_to_all(part, ("z", "core"), 0, 0, tiled=True)
     beyond = lax.ppermute(window, GRID, [((i + 1) % blocks, i) for i in range(blocks)])
-    (sens,) = call(
-        adjoint, [shape(8, 8, 256)], low, own, window, beyond, k, joined, follows
-    )
-    final = functools.partial(newton_step, count)
-    final.__name__ = "newton_step"
-    factor, newton = call(final, [shape(64, 64), shape(1, 64)], parts, wide)
+    last = functools.partial(finish, count)
+    last.__name__ = "finish"
+    factor, newton, sens = call(
+        last,
+        [shape(64, 64), shape(1, 64), shape(8, 8, 256)],
+        parts,
+        wide,
+        low,
+        own,
+        window,
+        beyond,
+        k,
+        joined,
+        follows,
+    )
     return factor, newton.reshape(64), sens.reshape(8, 1, 8, 256)
 
 

time: 80.8 us -> 81 us (level)
  waiting for transfers between devices: 16.3 us -> 17.5 us
  Pallas kernels: 6.53 us -> 5.52 us
    all_to_all x1, waiting for transfers between devices: 1.16 us -> 2.43 us  [per_device(): parts = lax.all_to_all(part, ('z', 'core'), 0, 0, tiled=True)]
    pallas_call x7 -> x6, Pallas kernels: 6.53 us -> 5.52 us  [call(): pl.pallas_call(body, out_shape=outs, in_specs=[pl.BlockSpec(memory_space=...]
  transfers between devices with their start and end apart: 3 -> 3, of which waited for: 3 -> 3; matrix products, arithmetic and copies ran while one was open for 0% -> 0% of each run, Pallas kernels for 2% -> 0%
where the time goes in v6:
time: 81 us; the launch traced here: 80.6 us
  blocking collectives  40.8 us (50%)
  waiting for transfers between devices  17.5 us (22%)
  starting transfers between devices  15.4 us (19%)
  Pallas kernels  5.52 us (7%)
  between operations  1.38 us (2%)
    all_to_all x1, blocking collectives, per_device(): parts = lax.all_to_all(part, ('core', 'y'), 0, 0, tiled=True)  21.9 us
    ppermute x1, waiting for transfers between devices, per_device(): lax.ppermute(own, GRID, [(i, (i + 1) % blocks) for i in range(blocks)])  11.6 us
    all_to_all x1, blocking collectives, per_device(): field = lax.all_to_all(evolved, 'y', 0, 0, tiled=True)  9.6 us
    all_to_all x1, blocking collectives, per_device(): parts = lax.all_to_all(part, 'x', 0, 0, tiled=True)  9.28 us
    all_to_all x1, starting transfers between devices, per_device(): parts = lax.all_to_all(part, ('z', 'core'), 0, 0, tiled=True)  8.91 us
    pallas_call x6, Pallas kernels, call(): pl.pallas_call(body, out_shape=outs, in_specs=[pl.BlockSpec(memory_space=...  5.52 us
    ppermute x1, starting transfers between devices, per_device(): lax.ppermute(own, GRID, [(i, (i + 1) % blocks) for i in range(blocks)])  4.5 us
    ppermute x1, waiting for transfers between devices, per_device(): lax.ppermute(window, GRID, [((i + 1) % blocks, i) for i in range(blocks)])  3.5 us
  transfers between devices with their start and end apart: 3, of which 3 were waited for; matrix products, arithmetic and copies ran while one was open for 0% of the time, Pallas kernels for 0%

profile of v6, /device:TPU:1, one launch (start us, length us, event | category | flops | bytes accessed | tf_op | source)
XLA Modules:
  0.0 80.6 jit_solution(5252527519318242610)
XLA Ops:
  0.6 1.0 %pack_block.1.own = f32[13,8,256]{2,1,0:T(8,128)S(1)} custom-call(f32[8,8,256]{2,1,0:T(8,128)} %bitcast.16, f32[16,256]{1,0:T(8,128)} %bitcast.17, s32[8,256]{1,0:T(8,128)} %col.1, f32[8,256]{1,0:T(8,128)} %bitcast.18, s32[8,8,8]{2,1,0:T(8,128)} %mask.1), custom_call_target="tpu_custom_call" | custom-call | flops 1000000 | bytes 206848 | tf_op jit(solution)/shard_map/pack_block/pallas_call | solution.py:26
  1.6 4.5 %collective-permute-start = (f32[13,8,256]{2,1,0:T(8,128)S(1)}, f32[13,8,256]{2,1,0:T(8,128)S(1)}, u32[]{:S(2)}, u32[]{:S(2)}) collective-permute-start(f32[13,8,256]{2,1,0:T(8,128)S(1)} %pack_block.1.own), channel_id=1, source_target_pairs={{0,8},{8,16},{16,24},{24,32},{32,40},{40,48},{48,56},{56,64},{64,7... | collective-permute-start | bytes 319496 | tf_op jit(solution)/shard_map/ppermute | solution.py:318
  6.1 0.0 copy-start
  6.8 0.0 copy-done
  6.8 11.6 %collective-permute-done.low = f32[13,8,256]{2,1,0:T(8,128)S(1)} collective-permute-done((f32[13,8,256]{2,1,0:T(8,128)S(1)}, f32[13,8,256]{2,1,0:T(8,128)S(1)}, u32[]{:S(2)}, u32[]{:S(2)}) %collective-permute-start) | collective-permute-done | bytes 106528 | tf_op jit(solution)/shard_map/ppermute | solution.py:318
  18.4 0.5 tangent.1
  18.9 9.6 %all_to_all.20.field = f32[8,8,256]{2,1,0:T(8,128)S(1)} all-to-all(f32[8,8,256]{2,1,0:T(8,128)S(1)} %get-tuple-element.11), channel_id=1, replica_groups=mesh['z'=8,'x'=8,'core'=2,'y'=8] {'y'}, dimensions={0} | all-to-all | bytes 131072 | tf_op jit(solution)/shard_map/all_to_all | solution.py:338
  28.5 0.3 gram_block.1
  28.9 21.9 %all_to_all.21.parts = f32[16,1,1408]{2,1,0:T(1,128)S(1)} all-to-all(f32[16,1,1408]{2,1,0:T(1,128)S(1)} %gram_block.1), channel_id=1, replica_groups=mesh['z'=8,'x'=8,'core'=2,'y'=8] {'core','y'}, dimensions={0} | all-to-all | bytes 180224 | tf_op jit(solution)/shard_map/all_to_all | solution.py:340
  50.8 0.1 first_sum.1
  50.9 9.3 %all_to_all.22.parts = f32[8,1,1152]{2,1,0:T(1,128)S(1)} all-to-all(f32[8,1,1152]{2,1,0:T(1,128)S(1)} %get-tuple-element.14), channel_id=1, replica_groups=mesh['z'=8,'x'=8,'core'=2,'y'=8] {'x'}, dimensions={0} | all-to-all | bytes 73728 | tf_op jit(solution)/shard_map/all_to_all | solution.py:348
  60.1 0.6 next_sum.1
  60.8 8.9 %all-to-all-start.3 = ((f32[16,1,1152]{2,1,0:T(1,128)}), f32[16,1,1152]{2,1,0:T(1,128)S(1)}, u32[]{:S(2)}, u32[]{:S(2)}) async-start(f32[16,1,1152]{2,1,0:T(1,128)} %next_sum.1), calls=%async_computation.3 | async-start | bytes 147456 | tf_op jit(solution)/shard_map/all_to_all | solution.py:350
  69.7 2.0 %collective-permute-start.1 = (f32[4,8,256]{2,1,0:T(8,128)S(1)}, f32[4,8,256]{2,1,0:T(8,128)S(1)}, u32[]{:S(2)}, u32[]{:S(2)}) collective-permute-start(f32[4,8,256]{2,1,0:T(8,128)S(1)} %get-tuple-element.15.window), channel_id=1, source_target_pairs={{8,0},{16,8},{24,16},{32,24},{40,32},{48,40},{56,48},{64,56},{72,6... | collective-permute-start | bytes 98312 | tf_op jit(solution)/shard_map/ppermute | solution.py:351
  71.7 3.5 %collective-permute-done.1.beyond = f32[4,8,256]{2,1,0:T(8,128)S(1)} collective-permute-done((f32[4,8,256]{2,1,0:T(8,128)S(1)}, f32[4,8,256]{2,1,0:T(8,128)S(1)}, u32[]{:S(2)}, u32[]{:S(2)}) %collective-permute-start.1) | collective-permute-done | bytes 32800 | tf_op jit(solution)/shard_map/ppermute | solution.py:351
  75.2 2.4 %all-to-all-done.3.parts = f32[16,1,1152]{2,1,0:T(1,128)S(1)} async-done(((f32[16,1,1152]{2,1,0:T(1,128)}), f32[16,1,1152]{2,1,0:T(1,128)S(1)}, u32[]{:S(2)}, u32[]{:S(2)}) %all-to-all-start.3) | async-done | bytes 73760 | tf_op jit(solution)/shard_map/all_to_all | solution.py:350
  77.6 3.0 %finish.1 = (f32[64,64]{1,0:T(8,128)}, f32[1,64]{1,0:T(1,128)}, f32[8,8,256]{2,1,0:T(8,128)}) custom-call(f32[16,1,1152]{2,1,0:T(1,128)S(1)} %all-to-all-done.3.parts, f32[1,128]{1,0:T(1,128)S(1)} %pad_bitcast_fusion.alpha, f32[13,8,256]{2,1,0:T(8,128)S(1)} %collective-permute-done.low, f32[13,8,256]{2,1,0:T(8,128)S(1)} %pack_block.1.own, ...), custom_call_target="tpu_custom_call" | custom-call | flops 1000000 | bytes 434956 | tf_op jit(solution)/shard_map/finish/pallas_call | solution.py:26
  (1 shorter events, 0.0 us)
Async XLA Ops:
  1.6 16.8 %collective-permute-start = (f32[13,8,256]{2,1,0:T(8,128)S(1)}, f32[13,8,256]{2,1,0:T(8,128)S(1)}, u32[]{:S(2)}, u32[]{:S(2)}) collective-permute-start(f32[13,8,256]{2,1,0:T(8,128)S(1)} %pack_block.1.own), channel_id=1, source_target_pairs={{0,8},{8,16},{16,24},{24,32},{32,40},{40,48},{48,56},{56,64},{64,7... | collective-permute-start | bytes 319496 | tf_op jit(solution)/shard_map/ppermute | solution.py:318
  6.1 0.7 copy-start
  60.8 16.8 %all-to-all-start.3 = ((f32[16,1,1152]{2,1,0:T(1,128)}), f32[16,1,1152]{2,1,0:T(1,128)S(1)}, u32[]{:S(2)}, u32[]{:S(2)}) async-start(f32[16,1,1152]{2,1,0:T(1,128)} %next_sum.1), calls=%async_computation.3 | async-start | bytes 147456 | tf_op jit(solution)/shard_map/all_to_all | solution.py:350
  69.7 5.5 %collective-permute-start.1 = (f32[4,8,256]{2,1,0:T(8,128)S(1)}, f32[4,8,256]{2,1,0:T(8,128)S(1)}, u32[]{:S(2)}, u32[]{:S(2)}) collective-permute-start(f32[4,8,256]{2,1,0:T(8,128)S(1)} %get-tuple-element.15.window), channel_id=1, source_target_pairs={{8,0},{16,8},{24,16},{32,24},{40,32},{48,40},{56,48},{64,56},{72,6... | collective-permute-start | bytes 98312 | tf_op jit(solution)/shard_map/ppermute | solution.py:351

commit v7 on v5

--- a/solution.py
+++ b/solution.py
@@ -43,7 +43,7 @@
     return lax.broadcasted_iota(jnp.int32, dims, axis)
 
 
-def pack_block(field, winds, col, innov, mask, out, *scratch):
+def pack_block(field, winds, col, innov, mask, out, near, *scratch):
     held, sems = scratch[:5], scratch[5]
     copies = [
         pltpu.make_async_copy(source, target, sems.at[n])
@@ -51,16 +51,20 @@
     ]
     for copy in copies:
         copy.start()
-    for copy in copies:
-        copy.wait()
-    out[0:8] = jnp.swapaxes(held[0][...], 0, 1)
+    for n in (2, 3, 1, 4):
+        copies[n].wait()
+    near[0, 4:8, :] = held[2][0:4, :].astype(F32)
+    near[1, 4:8, :] = held[3][0:4, :]
+    near[:, 0:4, :] = jnp.zeros((2, 4, 256), F32)
     out[8] = held[1][0:8, :]
     out[9] = held[1][8:16, :]
-    out[10] = held[2][...].astype(F32)
-    out[11] = held[3][...]
-    out[12] = jnp.zeros((8, 256), F32)
+    out[10, 0:4, :] = held[2][4:8, :].astype(F32)
+    out[10, 4:8, :] = held[3][4:8, :]
+    out[11] = jnp.zeros((8, 256), F32)
     for m in range(8):
-        out[12, :, 8 * m : 8 * m + 8] = held[4][m].astype(F32)
+        out[11, :, 8 * m : 8 * m + 8] = held[4][m].astype(F32)
+    copies[0].wait()
+    out[0:8] = jnp.swapaxes(held[0][...], 0, 1)
 
 
 def east(x):
@@ -81,7 +85,7 @@
     return jnp.sum(jnp.where(sub == mine, tile, 0.0), axis=0, keepdims=True)
 
 
-def tangent(low, own, kappa, mine, joined, alpha, core, follows, out, binned, column_of):
+def tangent(low, own, near, kappa, mine, joined, alpha, core, follows, out, binned, column_of):
     column_of[...] = jnp.transpose(jnp.broadcast_to(alpha[...], (128, 128)))[0:64]
     blocks = (low, own)
     k = jnp.broadcast_to(kappa[...], (8, 256))
@@ -106,10 +110,10 @@
     for y in range(8):
         out[y] = rows[4 + y]
     sub = iota2((8, 256), 0)
-    turned = [
-        jnp.where(sub < 4, pltpu.roll(low[tile], 4, 0), pltpu.roll(own[tile], 4, 0))
-        for tile in (10, 11)
-    ]
+    turned = (
+        jnp.where(sub < 4, low[10], near[0]),
+        jnp.where(sub < 4, pltpu.roll(low[10], 4, 0), near[1]),
+    )
     column, value = (select_row(tile, sub, mine[...]) for tile in turned)
     hit = (iota2((256, 256), 0).astype(F32) == column).astype(F32)
     values = jnp.where(sub == 0, 1.0, jnp.broadcast_to(value, (8, 256)))
@@ -122,7 +126,7 @@
     k = jnp.broadcast_to(kappa[...], (8, 256))
     below = jnp.broadcast_to(joined[...], (8, 256))
     above = jnp.broadcast_to(follows[...], (8, 256))
-    masks = jnp.concatenate([b[:, 0:128] for b in (low[12], own[12], beyond[3])], axis=0)
+    masks = jnp.concatenate([b[:, 0:128] for b in (low[11], own[11], beyond[3])], axis=0)
     wide = []
     for m in range(8):
         expand = (iota2((128, 256), 0) == 8 * m + iota2((128, 256), 1) // 32).astype(F32)
@@ -210,7 +214,7 @@
         )
     window[1] = own[8]
     window[2] = own[9]
-    window[3] = own[12]
+    window[3] = own[11]
 
 
 def next_sum(parts, out):
@@ -300,9 +304,9 @@
         innov.reshape(8, 256),
         loc_mask,
     )
-    (own,) = call(
+    own, near = call(
         pack_block,
-        [shape(13, 8, 256)],
+        [shape(12, 8, 256), shape(2, 8, 256)],
         *(pltpu.with_memory_space_constraint(a, pltpu.HBM) for a in sources),
         space=pltpu.HBM,
         scratch=[pltpu.VMEM(a.shape, a.dtype) for a in sources]
@@ -321,6 +325,7 @@
         [shape(8, 8, 256), shape(8, 256), shape(64, 128)],
         low,
         own,
+        near,
         k,
         mine,
         joined,

time: 80.8 us -> 80.7 us (level)
  no operation moved by 1% of the time
where the time goes in v7:
time: 80.7 us; the launch traced here: 80.3 us
  blocking collectives  40.7 us (50%)
  waiting for transfers between devices  16.3 us (20%)
  starting transfers between devices  15.4 us (19%)
  Pallas kernels  6.54 us (8%)
  between operations  1.38 us (2%)
    all_to_all x1, blocking collectives, per_device(): parts = lax.all_to_all(part, ('core', 'y'), 0, 0, tiled=True)  21.8 us
    ppermute x1, waiting for transfers between devices, per_device(): lax.ppermute(own, GRID, [(i, (i + 1) % blocks) for i in range(blocks)])  11.6 us
    all_to_all x1, blocking collectives, per_device(): field = lax.all_to_all(evolved, 'y', 0, 0, tiled=True)  9.6 us
    all_to_all x1, blocking collectives, per_device(): parts = lax.all_to_all(part, 'x', 0, 0, tiled=True)  9.28 us
    all_to_all x1, starting transfers between devices, per_device(): parts = lax.all_to_all(part, ('z', 'core'), 0, 0, tiled=True)  8.91 us
    pallas_call x7, Pallas kernels, call(): pl.pallas_call(body, out_shape=outs, in_specs=[pl.BlockSpec(memory_space=...  6.54 us
    ppermute x1, starting transfers between devices, per_device(): lax.ppermute(own, GRID, [(i, (i + 1) % blocks) for i in range(blocks)])  4.5 us
    ppermute x1, waiting for transfers between devices, per_device(): lax.ppermute(window, GRID, [((i + 1) % blocks, i) for i in range(blocks)])  3.5 us
  transfers between devices with their start and end apart: 3, of which 3 were waited for; matrix products, arithmetic and copies ran while one was open for 0% of the time, Pallas kernels for 2%

profile of v7, /device:TPU:1, one launch (start us, length us, event | category | flops | bytes accessed | tf_op | source)
XLA Modules:
  0.0 80.3 jit_solution(6035153442514439133)
XLA Ops:
  0.6 1.0 %pack_block.1 = (f32[12,8,256]{2,1,0:T(8,128)S(1)}, f32[2,8,256]{2,1,0:T(8,128)S(1)}) custom-call(f32[8,8,256]{2,1,0:T(8,128)} %bitcast.17, f32[16,256]{1,0:T(8,128)} %bitcast.18, s32[8,256]{1,0:T(8,128)} %col.1, f32[8,256]{1,0:T(8,128)} %bitcast.19, s32[8,8,8]{2,1,0:T(8,128)} %mask.1), custom_call_target="tpu_custom_call" | custom-call | flops 1000000 | bytes 215040 | tf_op jit(solution)/shard_map/pack_block/pallas_call | solution.py:26
  1.6 4.5 %collective-permute-start = (f32[12,8,256]{2,1,0:T(8,128)S(1)}, f32[12,8,256]{2,1,0:T(8,128)S(1)}, u32[]{:S(2)}, u32[]{:S(2)}) collective-permute-start(f32[12,8,256]{2,1,0:T(8,128)S(1)} %get-tuple-element.12.own), channel_id=1, source_target_pairs={{0,8},{8,16},{16,24},{24,32},{32,40},{40,48},{48,56},{56,64},{64,7... | collective-permute-start | bytes 294920 | tf_op jit(solution)/shard_map/ppermute | solution.py:315
  6.1 0.0 copy-start
  6.8 0.0 copy-done
  6.8 11.6 %collective-permute-done.low = f32[12,8,256]{2,1,0:T(8,128)S(1)} collective-permute-done((f32[12,8,256]{2,1,0:T(8,128)S(1)}, f32[12,8,256]{2,1,0:T(8,128)S(1)}, u32[]{:S(2)}, u32[]{:S(2)}) %collective-permute-start) | collective-permute-done | bytes 98336 | tf_op jit(solution)/shard_map/ppermute | solution.py:315
  18.4 0.5 tangent.1
  18.9 9.6 %all_to_all.20.field = f32[8,8,256]{2,1,0:T(8,128)S(1)} all-to-all(f32[8,8,256]{2,1,0:T(8,128)S(1)} %get-tuple-element.14), channel_id=1, replica_groups=mesh['z'=8,'x'=8,'core'=2,'y'=8] {'y'}, dimensions={0} | all-to-all | bytes 131072 | tf_op jit(solution)/shard_map/all_to_all | solution.py:336
  28.5 0.3 gram_block.1
  28.8 21.8 %all_to_all.21.parts = f32[16,1,1408]{2,1,0:T(1,128)S(1)} all-to-all(f32[16,1,1408]{2,1,0:T(1,128)S(1)} %gram_block.1), channel_id=1, replica_groups=mesh['z'=8,'x'=8,'core'=2,'y'=8] {'core','y'}, dimensions={0} | all-to-all | bytes 180224 | tf_op jit(solution)/shard_map/all_to_all | solution.py:338
  50.7 0.1 first_sum.1
  50.8 9.3 %all_to_all.22.parts = f32[8,1,1152]{2,1,0:T(1,128)S(1)} all-to-all(f32[8,1,1152]{2,1,0:T(1,128)S(1)} %get-tuple-element.17), channel_id=1, replica_groups=mesh['z'=8,'x'=8,'core'=2,'y'=8] {'x'}, dimensions={0} | all-to-all | bytes 73728 | tf_op jit(solution)/shard_map/all_to_all | solution.py:346
  60.0 0.6 next_sum.1
  60.7 8.9 %all-to-all-start.3 = ((f32[16,1,1152]{2,1,0:T(1,128)}), f32[16,1,1152]{2,1,0:T(1,128)S(1)}, u32[]{:S(2)}, u32[]{:S(2)}) async-start(f32[16,1,1152]{2,1,0:T(1,128)} %next_sum.1), calls=%async_computation.3 | async-start | bytes 147456 | tf_op jit(solution)/shard_map/all_to_all | solution.py:348
  69.6 2.0 %collective-permute-start.1 = (f32[4,8,256]{2,1,0:T(8,128)S(1)}, f32[4,8,256]{2,1,0:T(8,128)S(1)}, u32[]{:S(2)}, u32[]{:S(2)}) collective-permute-start(f32[4,8,256]{2,1,0:T(8,128)S(1)} %get-tuple-element.20.window), channel_id=1, source_target_pairs={{8,0},{16,8},{24,16},{32,24},{40,32},{48,40},{56,48},{64,56},{72,6... | collective-permute-start | bytes 98312 | tf_op jit(solution)/shard_map/ppermute | solution.py:349
  71.6 3.5 %collective-permute-done.1.beyond = f32[4,8,256]{2,1,0:T(8,128)S(1)} collective-permute-done((f32[4,8,256]{2,1,0:T(8,128)S(1)}, f32[4,8,256]{2,1,0:T(8,128)S(1)}, u32[]{:S(2)}, u32[]{:S(2)}) %collective-permute-start.1) | collective-permute-done | bytes 32800 | tf_op jit(solution)/shard_map/ppermute | solution.py:349
  75.1 1.3 %adjoint.1 = f32[8,8,256]{2,1,0:T(8,128)} custom-call(f32[12,8,256]{2,1,0:T(8,128)S(1)} %collective-permute-done.low, f32[12,8,256]{2,1,0:T(8,128)S(1)} %get-tuple-element.12.own, f32[4,8,256]{2,1,0:T(8,128)S(1)} %get-tuple-element.20.window, f32[4,8,256]{2,1,0:T(8,128)S(1)} %collective-permute-done.1.beyond, f32[1,1]{1,0:T(1,128)} %bitcast.15.kappa, ...), custom_call_target="tpu_custom_call" | custom-call | flops 1000000 | bytes 327692 | tf_op jit(solution)/shard_map/adjoint/pallas_call | solution.py:26
  76.4 1.2 %all-to-all-done.3.parts = f32[16,1,1152]{2,1,0:T(1,128)S(1)} async-done(((f32[16,1,1152]{2,1,0:T(1,128)}), f32[16,1,1152]{2,1,0:T(1,128)S(1)}, u32[]{:S(2)}, u32[]{:S(2)}) %all-to-all-start.3) | async-done | bytes 73760 | tf_op jit(solution)/shard_map/all_to_all | solution.py:348
  77.5 2.8 %newton_step.1 = (f32[64,64]{1,0:T(8,128)}, f32[1,64]{1,0:T(1,128)}) custom-call(f32[16,1,1152]{2,1,0:T(1,128)S(1)} %all-to-all-done.3.parts, f32[1,128]{1,0:T(1,128)S(1)} %pad_bitcast_fusion.alpha), custom_call_target="tpu_custom_call" | custom-call | flops 1000000 | bytes 90880 | tf_op jit(solution)/shard_map/newton_step/pallas_call | solution.py:26
  (1 shorter events, 0.0 us)
Async XLA Ops:
  1.6 16.8 %collective-permute-start = (f32[12,8,256]{2,1,0:T(8,128)S(1)}, f32[12,8,256]{2,1,0:T(8,128)S(1)}, u32[]{:S(2)}, u32[]{:S(2)}) collective-permute-start(f32[12,8,256]{2,1,0:T(8,128)S(1)} %get-tuple-element.12.own), channel_id=1, source_target_pairs={{0,8},{8,16},{16,24},{24,32},{32,40},{40,48},{48,56},{56,64},{64,7... | collective-permute-start | bytes 294920 | tf_op jit(solution)/shard_map/ppermute | solution.py:315
  6.1 0.7 copy-start
  60.7 16.9 %all-to-all-start.3 = ((f32[16,1,1152]{2,1,0:T(1,128)}), f32[16,1,1152]{2,1,0:T(1,128)S(1)}, u32[]{:S(2)}, u32[]{:S(2)}) async-start(f32[16,1,1152]{2,1,0:T(1,128)} %next_sum.1), calls=%async_computation.3 | async-start | bytes 147456 | tf_op jit(solution)/shard_map/all_to_all | solution.py:348
  69.6 5.5 %collective-permute-start.1 = (f32[4,8,256]{2,1,0:T(8,128)S(1)}, f32[4,8,256]{2,1,0:T(8,128)S(1)}, u32[]{:S(2)}, u32[]{:S(2)}) collective-permute-start(f32[4,8,256]{2,1,0:T(8,128)S(1)} %get-tuple-element.20.window), channel_id=1, source_target_pairs={{8,0},{16,8},{24,16},{32,24},{40,32},{48,40},{56,48},{64,56},{72,6... | collective-permute-start | bytes 98312 | tf_op jit(solution)/shard_map/ppermute | solution.py:349

commit v8 on v7

--- a/solution.py
+++ b/solution.py
@@ -14,7 +14,7 @@
 GRID = ("z", "x", "core")
 CORE = 17 * 128
 HALF = 9 * 128
-PACK = HALF + 256
+PACK = CORE + 256
 
 
 def vmem():
@@ -85,7 +85,7 @@
     return jnp.sum(jnp.where(sub == mine, tile, 0.0), axis=0, keepdims=True)
 
 
-def tangent(low, own, near, kappa, mine, joined, alpha, core, follows, out, binned, column_of):
+def tangent(low, own, near, kappa, mine, joined, alpha, follows, out, binned, column_of):
     column_of[...] = jnp.transpose(jnp.broadcast_to(alpha[...], (128, 128)))[0:64]
     blocks = (low, own)
     k = jnp.broadcast_to(kappa[...], (8, 256))
@@ -190,9 +190,9 @@
     diagonal = jnp.sum(jnp.where(on_diagonal, g[32:64], 0.0), axis=0, keepdims=True)
     extra = jnp.where(iota2((1, 128), 1) < 64, g[64:65], diagonal)
     lines = [packed[r : r + 1] for r in range(16)] + [extra]
-    halves = [jnp.concatenate(lines[h : h + 9] + [forcing], axis=1) for h in (0, 8)]
+    flat = jnp.concatenate(lines + [forcing], axis=1)
     for c in range(copies):
-        out[c] = halves[2 * c // copies]
+        out[c] = flat
 
 
 def sum_blocks(parts, first=0, stride=1):
@@ -202,16 +202,13 @@
     return total
 
 
-def first_sum(parts, own, core, out, window):
-    half = parts.shape[0] // 2
-    total = sum_blocks(parts)[:, 0:HALF]
+def first_sum(parts, own, out, window):
+    total = sum_blocks(parts)
+    halves = (total[:, 0:HALF], total[:, CORE - HALF : CORE])
     for c in range(out.shape[0]):
-        out[c] = total
-    odd = core[...] > 0.5
+        out[c] = halves[c % 2]
     for y in range(8):
-        window[0, y : y + 1, :] = jnp.where(
-            odd, parts[half + y][:, HALF:PACK], parts[y][:, HALF:PACK]
-        )
+        window[0, y : y + 1, :] = parts[y][:, CORE:PACK]
     window[1] = own[8]
     window[2] = own[9]
     window[3] = own[11]
@@ -314,7 +311,6 @@
     )
     low = lax.ppermute(own, GRID, [(i, (i + 1) % blocks) for i in range(blocks)])
     index = lax.axis_index(GRID)
-    core = lax.axis_index("core").astype(F32).reshape(1, 1)
     joined = (index > 0).astype(F32).reshape(1, 1)
     follows = (index < blocks - 1).astype(F32).reshape(1, 1)
     mine = lax.axis_index("y").reshape(1, 1)
@@ -330,20 +326,18 @@
         mine,
         joined,
         wide,
-        core,
         follows,
     )
     field = lax.all_to_all(evolved, "y", 0, 0, tiled=True)
-    (part,) = call(gram_block, [shape(2 * ny, 1, PACK)], field, binned, column)
-    parts = lax.all_to_all(part, ("core", "y"), 0, 0, tiled=True)
+    (part,) = call(gram_block, [shape(ny, 1, PACK)], field, binned, column)
+    parts = lax.all_to_all(part, "y", 0, 0, tiled=True)
     part, window = call(
         first_sum,
-        [shape(lax.axis_size("x"), 1, HALF), shape(4, 8, 256)],
+        [shape(2 * lax.axis_size("x"), 1, HALF), shape(4, 8, 256)],
         parts,
         own,
-        core,
-    )
-    parts = lax.all_to_all(part, "x", 0, 0, tiled=True)
+    )
+    parts = lax.all_to_all(part, ("x", "core"), 0, 0, tiled=True)
     (part,) = call(next_sum, [shape(2 * lax.axis_size("z"), 1, HALF)], parts)
     parts = lax.all_to_all(part, ("z", "core"), 0, 0, tiled=True)
     beyond = lax.ppermute(window, GRID, [((i + 1) % blocks, i) for i in range(blocks)])

time: 80.7 us -> 80.8 us (level)
  blocking collectives: 40.7 us -> 43 us
  starting transfers between devices: 15.4 us -> 13.2 us
    all_to_all x2, blocking collectives: 31.1 us -> 33.4 us  [the longest x1 23.7 us: per_device(): parts = lax.all_to_all(part, ('x', 'core'), 0, 0, tiled=True)]
    all_to_all x1, starting transfers between devices: 8.91 us -> 6.72 us  [per_device(): parts = lax.all_to_all(part, ('z', 'core'), 0, 0, tiled=True)]
where the time goes in v8:
time: 80.8 us; the launch traced here: 80.4 us
  blocking collectives  43 us (53%)
  waiting for transfers between devices  16.3 us (20%)
  starting transfers between devices  13.2 us (16%)
  Pallas kernels  6.48 us (8%)
  between operations  1.38 us (2%)
    all_to_all x1, blocking collectives, per_device(): parts = lax.all_to_all(part, ('x', 'core'), 0, 0, tiled=True)  23.7 us
    ppermute x1, waiting for transfers between devices, per_device(): lax.ppermute(own, GRID, [(i, (i + 1) % blocks) for i in range(blocks)])  11.6 us
    all_to_all x1, blocking collectives, per_device(): parts = lax.all_to_all(part, 'y', 0, 0, tiled=True)  9.75 us
    all_to_all x1, blocking collectives, per_device(): field = lax.all_to_all(evolved, 'y', 0, 0, tiled=True)  9.6 us
    all_to_all x1, starting transfers between devices, per_device(): parts = lax.all_to_all(part, ('z', 'core'), 0, 0, tiled=True)  6.72 us
    pallas_call x7, Pallas kernels, call(): pl.pallas_call(body, out_shape=outs, in_specs=[pl.BlockSpec(memory_space=...  6.48 us
    ppermute x1, starting transfers between devices, per_device(): lax.ppermute(own, GRID, [(i, (i + 1) % blocks) for i in range(blocks)])  4.5 us
    ppermute x1, waiting for transfers between devices, per_device(): lax.ppermute(window, GRID, [((i + 1) % blocks, i) for i in range(blocks)])  3.5 us
  transfers between devices with their start and end apart: 3, of which 3 were waited for; matrix products, arithmetic and copies ran while one was open for 0% of the time, Pallas kernels for 2%

profile of v8, /device:TPU:1, one launch (start us, length us, event | category | flops | bytes accessed | tf_op | source)
XLA Modules:
  0.0 80.4 jit_solution(14942202750569455678)
XLA Ops:
  0.6 1.0 %pack_block.1 = (f32[12,8,256]{2,1,0:T(8,128)S(1)}, f32[2,8,256]{2,1,0:T(8,128)S(1)}) custom-call(f32[8,8,256]{2,1,0:T(8,128)} %bitcast.16, f32[16,256]{1,0:T(8,128)} %bitcast.17, s32[8,256]{1,0:T(8,128)} %col.1, f32[8,256]{1,0:T(8,128)} %bitcast.18, s32[8,8,8]{2,1,0:T(8,128)} %mask.1), custom_call_target="tpu_custom_call" | custom-call | flops 1000000 | bytes 215040 | tf_op jit(solution)/shard_map/pack_block/pallas_call | solution.py:26
  1.6 4.5 %collective-permute-start = (f32[12,8,256]{2,1,0:T(8,128)S(1)}, f32[12,8,256]{2,1,0:T(8,128)S(1)}, u32[]{:S(2)}, u32[]{:S(2)}) collective-permute-start(f32[12,8,256]{2,1,0:T(8,128)S(1)} %get-tuple-element.12.own), channel_id=1, source_target_pairs={{0,8},{8,16},{16,24},{24,32},{32,40},{40,48},{48,56},{56,64},{64,7... | collective-permute-start | bytes 294920 | tf_op jit(solution)/shard_map/ppermute | solution.py:312
  6.1 0.0 copy-start
  6.8 0.0 copy-done
  6.8 11.6 %collective-permute-done.low = f32[12,8,256]{2,1,0:T(8,128)S(1)} collective-permute-done((f32[12,8,256]{2,1,0:T(8,128)S(1)}, f32[12,8,256]{2,1,0:T(8,128)S(1)}, u32[]{:S(2)}, u32[]{:S(2)}) %collective-permute-start) | collective-permute-done | bytes 98336 | tf_op jit(solution)/shard_map/ppermute | solution.py:312
  18.4 0.5 tangent.1
  18.9 9.6 %all_to_all.20.field = f32[8,8,256]{2,1,0:T(8,128)S(1)} all-to-all(f32[8,8,256]{2,1,0:T(8,128)S(1)} %get-tuple-element.14), channel_id=1, replica_groups=mesh['z'=8,'x'=8,'core'=2,'y'=8] {'y'}, dimensions={0} | all-to-all | bytes 131072 | tf_op jit(solution)/shard_map/all_to_all | solution.py:331
  28.5 0.3 gram_block.1
  28.8 9.7 %all_to_all.21.parts = f32[8,1,2432]{2,1,0:T(1,128)S(1)} all-to-all(f32[8,1,2432]{2,1,0:T(1,128)S(1)} %gram_block.1), channel_id=1, replica_groups=mesh['z'=8,'x'=8,'core'=2,'y'=8] {'y'}, dimensions={0} | all-to-all | bytes 155648 | tf_op jit(solution)/shard_map/all_to_all | solution.py:333
  38.6 23.7 %all_to_all.22.parts = f32[16,1,1152]{2,1,0:T(1,128)S(1)} all-to-all(f32[16,1,1152]{2,1,0:T(1,128)S(1)} %get-tuple-element.17), channel_id=1, replica_groups=mesh['z'=8,'x'=8,'core'=2,'y'=8] {'x','core'}, dimensions={0} | all-to-all | bytes 147456 | tf_op jit(solution)/shard_map/all_to_all | solution.py:340
  62.3 0.7 next_sum.1
  63.0 6.7 %all-to-all-start.3 = ((f32[16,1,1152]{2,1,0:T(1,128)}), f32[16,1,1152]{2,1,0:T(1,128)S(1)}, u32[]{:S(2)}, u32[]{:S(2)}) async-start(f32[16,1,1152]{2,1,0:T(1,128)} %next_sum.1), calls=%async_computation.3 | async-start | bytes 147456 | tf_op jit(solution)/shard_map/all_to_all | solution.py:342
  69.7 2.0 %collective-permute-start.1 = (f32[4,8,256]{2,1,0:T(8,128)S(1)}, f32[4,8,256]{2,1,0:T(8,128)S(1)}, u32[]{:S(2)}, u32[]{:S(2)}) collective-permute-start(f32[4,8,256]{2,1,0:T(8,128)S(1)} %get-tuple-element.20.window), channel_id=1, source_target_pairs={{8,0},{16,8},{24,16},{32,24},{40,32},{48,40},{56,48},{64,56},{72,6... | collective-permute-start | bytes 98312 | tf_op jit(solution)/shard_map/ppermute | solution.py:343
  71.7 3.5 %collective-permute-done.1.beyond = f32[4,8,256]{2,1,0:T(8,128)S(1)} collective-permute-done((f32[4,8,256]{2,1,0:T(8,128)S(1)}, f32[4,8,256]{2,1,0:T(8,128)S(1)}, u32[]{:S(2)}, u32[]{:S(2)}) %collective-permute-start.1) | collective-permute-done | bytes 32800 | tf_op jit(solution)/shard_map/ppermute | solution.py:343
  75.2 1.3 %adjoint.1 = f32[8,8,256]{2,1,0:T(8,128)} custom-call(f32[12,8,256]{2,1,0:T(8,128)S(1)} %collective-permute-done.low, f32[12,8,256]{2,1,0:T(8,128)S(1)} %get-tuple-element.12.own, f32[4,8,256]{2,1,0:T(8,128)S(1)} %get-tuple-element.20.window, f32[4,8,256]{2,1,0:T(8,128)S(1)} %collective-permute-done.1.beyond, f32[1,1]{1,0:T(1,128)} %bitcast.14.kappa, ...), custom_call_target="tpu_custom_call" | custom-call | flops 1000000 | bytes 327692 | tf_op jit(solution)/shard_map/adjoint/pallas_call | solution.py:26
  76.5 1.2 %all-to-all-done.3.parts = f32[16,1,1152]{2,1,0:T(1,128)S(1)} async-done(((f32[16,1,1152]{2,1,0:T(1,128)}), f32[16,1,1152]{2,1,0:T(1,128)S(1)}, u32[]{:S(2)}, u32[]{:S(2)}) %all-to-all-start.3) | async-done | bytes 73760 | tf_op jit(solution)/shard_map/all_to_all | solution.py:342
  77.6 2.8 %newton_step.1 = (f32[64,64]{1,0:T(8,128)}, f32[1,64]{1,0:T(1,128)}) custom-call(f32[16,1,1152]{2,1,0:T(1,128)S(1)} %all-to-all-done.3.parts, f32[1,128]{1,0:T(1,128)S(1)} %pad_bitcast_fusion.alpha), custom_call_target="tpu_custom_call" | custom-call | flops 1000000 | bytes 90880 | tf_op jit(solution)/shard_map/newton_step/pallas_call | solution.py:26
  (2 shorter events, 0.0 us)
Async XLA Ops:
  1.6 16.8 %collective-permute-start = (f32[12,8,256]{2,1,0:T(8,128)S(1)}, f32[12,8,256]{2,1,0:T(8,128)S(1)}, u32[]{:S(2)}, u32[]{:S(2)}) collective-permute-start(f32[12,8,256]{2,1,0:T(8,128)S(1)} %get-tuple-element.12.own), channel_id=1, source_target_pairs={{0,8},{8,16},{16,24},{24,32},{32,40},{40,48},{48,56},{56,64},{64,7... | collective-permute-start | bytes 294920 | tf_op jit(solution)/shard_map/ppermute | solution.py:312
  6.1 0.7 copy-start
  63.0 14.7 %all-to-all-start.3 = ((f32[16,1,1152]{2,1,0:T(1,128)}), f32[16,1,1152]{2,1,0:T(1,128)S(1)}, u32[]{:S(2)}, u32[]{:S(2)}) async-start(f32[16,1,1152]{2,1,0:T(1,128)} %next_sum.1), calls=%async_computation.3 | async-start | bytes 147456 | tf_op jit(solution)/shard_map/all_to_all | solution.py:342
  69.7 5.5 %collective-permute-start.1 = (f32[4,8,256]{2,1,0:T(8,128)S(1)}, f32[4,8,256]{2,1,0:T(8,128)S(1)}, u32[]{:S(2)}, u32[]{:S(2)}) collective-permute-start(f32[4,8,256]{2,1,0:T(8,128)S(1)} %get-tuple-element.20.window), channel_id=1, source_target_pairs={{8,0},{16,8},{24,16},{32,24},{40,32},{48,40},{56,48},{64,56},{72,6... | collective-permute-start | bytes 98312 | tf_op jit(solution)/shard_map/ppermute | solution.py:343
